TPU v7x, 512 devices: a whole 4x4x16 slice. The times are simulated.
512 devices in a mesh: head: 32 (over x_lo, z), ctx: 8 (over y, core), dp: 2 (over x_hi).
Axes of the slice: x: 4 (x_hi: 2, x_lo: 2; x = x_hi * 2 + x_lo), y: 4, z: 16, core: 2. Of those that a mesh axis runs over, the one named last changes fastest.
Arguments:
- query_nope: bfloat16 [2, 1024, 128, 128], P('dp', 'ctx', 'head'), may hold values from -6 to 6
- query_rope: bfloat16 [2, 1024, 128, 64], P('dp', 'ctx', 'head'), may hold values from -10 to 10
- query_pos: int32 [2, 1024], P('dp', 'ctx'), may hold values from 64 to 1023
- latent_cache: bfloat16 [2, 16, 64, 576], P('dp', 'ctx'), may hold values from -6 to 6
- block_table: int32 [2, 16], P('dp'), may hold values from 0 to 15, each once within a row
- key_up: bfloat16 [128, 128, 512], P('head'), may hold values from -0.5 to 0.5
- value_up: bfloat16 [128, 512, 128], P('head'), may hold values from -0.25 to 0.25
- grad_out: bfloat16 [2, 1024, 128, 128], P('dp', 'ctx', 'head'), may hold values from -6 to 6
Outputs:
- grad_query_nope: float32 [2, 1024, 128, 128], P('dp', 'ctx', 'head')
- grad_query_rope: float32 [2, 1024, 128, 64], P('dp', 'ctx', 'head')
- grad_cache: float32 [2, 16, 64, 576], P('dp', 'ctx')
- grad_key_up: float32 [128, 128, 512], P('head', ('ctx', 'dp'))
- grad_value_up: float32 [128, 512, 128], P('head', ('ctx', 'dp'))
Inputs may be any that keep to these rules, and one draw needn't show every extreme that they name: Each row is a permutation: logical block b of sequence s lies in physical block block_table[s, b].
All inputs are finite; a program needn't handle non-finite values.
Results may differ from a plain program's by a relative error of at most 0.025.
Values may be sent and summed in bfloat16 or wider, within the bound.
A program may use at most 64 MiB of HBM per device.

v0:
```python
import jax
import jax.numpy as jnp
from jax import lax
from jax.sharding import PartitionSpec as P

softmax_scale = 192.0 ** (-0.5)
neg_big = -1e30


def on_device(
    query_nope, query_rope, query_pos, latent_cache, block_table, key_up, value_up, grad_out
):
    latent_width = key_up.shape[2]
    page_rows = latent_cache.shape[2]
    row_width = latent_cache.shape[3]
    query_latent = jnp.einsum(
        "qhn,hnl->hql", query_nope[0], key_up, preferred_element_type=jnp.float32
    ).astype(jnp.bfloat16)
    query_rows = jnp.concatenate([query_latent, jnp.swapaxes(query_rope[0], 0, 1)], axis=2)
    grad_latent = jnp.einsum(
        "qhv,hlv->hql", grad_out[0], value_up, preferred_element_type=jnp.float32
    ).astype(jnp.bfloat16)
    query_position = query_pos[0]
    slot_table = block_table[0]
    own_rows = latent_cache[0].reshape(-1, row_width)
    head_rows = query_rows.shape[0]
    query_count = query_rows.shape[1]

    def positions(row_count):
        row_index = jnp.arange(row_count, dtype=jnp.int32)
        slot_index = row_index // page_rows
        logical = jnp.sum(
            jnp.where(
                slot_table[None, :] == slot_index[:, None],
                jnp.arange(slot_table.shape[0], dtype=jnp.int32)[None, :],
                0,
            ),
            axis=1,
        )
        return logical * page_rows + row_index % page_rows

    def scores_of(key_block):
        raw_scores = (
            jnp.einsum("hqc,kc->hqk", query_rows, key_block, preferred_element_type=jnp.float32)
            * softmax_scale
        )
        visible = positions(key_block.shape[0])[None, None, :] <= query_position[None, :, None]
        return jnp.where(visible, raw_scores, -jnp.inf)

    def probs_grad(key_block):
        return jnp.einsum(
            "hql,kl->hqk",
            grad_latent,
            key_block[:, :latent_width],
            preferred_element_type=jnp.float32,
        )

    key_block = lax.all_gather(own_rows, "ctx", axis=0, tiled=True)
    stats_row_max = jnp.full((head_rows, query_count), neg_big, jnp.float32)
    scores = scores_of(key_block)
    grad_probs = probs_grad(key_block)
    new_max = jnp.maximum(stats_row_max, jnp.max(scores, axis=2))
    weights = jnp.exp(scores - new_max[..., None])
    denominator = jnp.sum(weights, axis=2)
    weighted_sum = jnp.sum(weights * grad_probs, axis=2)
    row_delta = weighted_sum / denominator
    key_block = lax.all_gather(own_rows, "ctx", axis=0, tiled=True)
    scores = scores_of(key_block)
    attn_probs = jnp.exp(scores - new_max[..., None]) / denominator[..., None]
    grad_probs = probs_grad(key_block)
    probs_b = attn_probs.astype(jnp.bfloat16)
    grad_scores = (attn_probs * (grad_probs - row_delta[..., None]) * softmax_scale).astype(
        jnp.bfloat16
    )
    grad_query = jnp.einsum(
        "hqk,kc->hqc", grad_scores, key_block, preferred_element_type=jnp.float32
    )
    out_part = jnp.einsum(
        "hqk,kl->hql", probs_b, key_block[:, :latent_width], preferred_element_type=jnp.float32
    )
    grad_rows = jnp.einsum(
        "hqk,hqc->kc", grad_scores, query_rows, preferred_element_type=jnp.float32
    )
    grad_values = jnp.einsum(
        "hqk,hql->kl", probs_b, grad_latent, preferred_element_type=jnp.float32
    )
    grad_rows = grad_rows + jnp.pad(grad_values, ((0, 0), (0, row_width - latent_width)))
    grad_query, out_part, grad_rows = (grad_query, out_part, grad_rows)
    grad_all = grad_rows
    grad_query, out_sum, grad_all = (grad_query, out_part, grad_all)
    attn_out = out_sum.astype(jnp.bfloat16)
    grad_rope = jnp.swapaxes(grad_query[..., latent_width:], 0, 1)[None]
    grad_qlatent = grad_query[..., :latent_width].astype(jnp.bfloat16)
    grad_nope = jnp.einsum(
        "hql,hnl->qhn", grad_qlatent, key_up, preferred_element_type=jnp.float32
    )[None]
    key_part = jnp.einsum(
        "qhn,hql->hnl", query_nope[0], grad_qlatent, preferred_element_type=jnp.float32
    ).astype(jnp.bfloat16)
    value_part = jnp.einsum(
        "hql,qhv->hlv", attn_out, grad_out[0], preferred_element_type=jnp.float32
    ).astype(jnp.bfloat16)
    grad_key_map, grad_value_map = (
        lax.psum_scatter(key_part, ("ctx", "dp"), scatter_dimension=1, tiled=True).astype(
            jnp.float32
        ),
        lax.psum_scatter(value_part, ("ctx", "dp"), scatter_dimension=1, tiled=True).astype(
            jnp.float32
        ),
    )
    ctx_share = lax.psum_scatter(
        grad_all.astype(jnp.bfloat16), "ctx", scatter_dimension=0, tiled=True
    )
    cache_grad = lax.psum(ctx_share, "head").astype(jnp.float32)
    return (
        grad_nope,
        grad_rope,
        cache_grad.reshape(latent_cache.shape),
        grad_key_map,
        grad_value_map,
    )


def solution(mesh):
    placed = (
        P("dp", "ctx", "head", None),
        P("dp", "ctx", "head", None),
        P("dp", "ctx"),
        P("dp", "ctx", None, None),
        P("dp", None),
        P("head", None, None),
        P("head", None, None),
        P("dp", "ctx", "head", None),
    )
    return jax.shard_map(
        on_device,
        mesh=mesh,
        in_specs=placed,
        out_specs=(
            P("dp", "ctx", "head", None),
            P("dp", "ctx", "head", None),
            P("dp", "ctx", None, None),
            P("head", ("ctx", "dp"), None),
            P("head", ("ctx", "dp"), None),
        ),
        check_vma=False,
    )
```

profile of v0, /device:TPU:6, one launch (start us, length us, event | category | flops | bytes accessed | tf_op | source)
XLA Modules:
  0.0 606.2 jit_solution(2296657191161061359)
XLA Ops:
  7.2 0.0 copy-start
  7.2 0.0 copy-start.2
  7.2 0.0 all-gather.2.cloned.1.call-start
  7.2 1.8 copy.60
  9.0 0.0 all-gather.2.cloned.1.call-update
  9.0 0.0 reduce-scatter.7.cloned.1.call-start
  9.1 1.0 copy.59
  10.1 0.7 select_reduce_fusion
  10.8 0.8 broadcast_compare_fusion
  11.6 0.0 copy-done
  11.6 1.2 convolution_convert_fusion.3
  12.8 0.0 copy-done.2
  12.8 1.2 convolution_convert_fusion.2
  14.0 32.4 %all-gather.2.cloned.1.call-done = bf16[1024,576]{0,1:T(8,128)(2,1)} async-done(((bf16[128,576]{0,1:T(8,128)(2,1)}), bf16[1024,576]{0,1:T(8,128)(2,1)}) %all-gather.2.cloned.1.call-update) | async-done | bytes 1179664 | tf_op jit(solution)/shard_map/all_gather | solution.py:67
  46.5 0.0 copy-start.5
  46.5 2.5 fusion.1
  49.0 0.0 copy-start.1
  49.0 0.0 copy-done.5
  49.0 1.1 fusion.8
  50.2 1.1 convolution_bitcast_fusion
  51.2 0.0 copy-done.1
  51.2 0.8 multiply_convert_fusion
  52.0 0.8 fusion
  52.9 1.5 copy.84
  54.3 0.0 reduce-scatter.7.cloned.1.call-update
  54.3 0.0 copy-start.3
  54.3 0.0 all-reduce.7.cloned.1.call-start
  54.4 2.1 fusion.3
  56.5 0.0 copy-done.3
  56.5 0.0 copy-start.4
  56.5 0.3 fusion.2
  56.8 1.2 copy.69
  58.0 0.0 all-reduce.7.cloned.1.call-update
  58.0 0.0 reduce-scatter.5.cloned.1.call-start
  58.1 0.0 copy-done.4
  58.1 3.7 convolution_convert_fusion
  61.8 0.0 reduce-scatter.5.cloned.1.call-update
  61.8 0.0 all-reduce.5.cloned.1.call-start
  61.9 1.3 dynamic-slice
  63.8 0.7 slice_bitcast_fusion.4
  64.5 31.3 %reduce-scatter.7.cloned.1.call-done = bf16[128,576]{1,0:T(8,128)(2,1)} async-done(((bf16[1024,576]{1,0:T(8,128)(2,1)}), bf16[128,576]{1,0:T(8,128)(2,1)}) %reduce-scatter.7.cloned.1.call-update) | async-done | bytes 147472 | tf_op jit(solution)/shard_map/reduce_scatter | solution.py:111
  95.7 0.0 all-reduce.5.cloned.1.call-update
  95.8 0.3 convolution_bitcast_fusion.1
  96.1 0.9 copy.73
  97.0 156.8 %all-reduce.7.cloned.1.call-done = bf16[4,128,512]{2,0,1:T(4,128)(2,1)} async-done(((bf16[4,128,512]{2,0,1:T(4,128)(2,1)}), bf16[4,128,512]{2,0,1:T(4,128)(2,1)}) %all-reduce.7.cloned.1.call-update) | async-done | bytes 524304
  253.8 0.8 dynamic-slice_convert_fusion
  254.6 0.7 copy.74
  255.2 91.8 %reduce-scatter.5.cloned.1.call-done = bf16[4,32,128]{2,1,0:T(8,128)(2,1)} async-done(((bf16[4,512,128]{2,1,0:T(8,128)(2,1)}), bf16[4,32,128]{2,1,0:T(8,128)(2,1)}) %reduce-scatter.5.cloned.1.call-update) | async-done | bytes 32784 | tf_op jit(solution)/shard_map/reduce_scatter | solution.py:107
  347.1 1.4 convert_element_type.47
  348.5 249.6 %all-reduce.5.cloned.1.call-done = bf16[1,2,64,576]{3,2,1,0:T(8,128)(2,1)} async-done(((bf16[1,2,64,576]{3,2,1,0:T(8,128)(2,1)}), bf16[1,2,64,576]{3,2,1,0:T(8,128)(2,1)}) %all-reduce.5.cloned.1.call-update) | async-done | bytes 147472 | tf_op jit(solution)/shard_map/psum | solution.py:114
  598.0 1.7 reshape.85
  (4 shorter events, 0.0 us)
Async XLA Ops:
  7.2 4.5 copy-start
  7.2 5.6 copy-start.2
  7.2 39.3 %all-gather.2.cloned.1.call-start = ((), (), s32[]{:S(2)}) async-start(), calls=%async_computation.2 | async-start | bytes 1327104 | tf_op jit(solution)/shard_map/all_gather | solution.py:67
  9.0 86.7 %reduce-scatter.7.cloned.1.call-start = ((), (), s32[]{:S(2)}) async-start(), calls=%async_computation.5 | async-start | bytes 1474560 | tf_op jit(solution)/shard_map/reduce_scatter | solution.py:111
  46.5 2.5 copy-start.5
  49.0 2.3 copy-start.1
  54.3 2.2 copy-start.3
  54.3 199.5 %all-reduce.7.cloned.1.call-start = ((), (), s32[]{:S(2)}) async-start(), calls=%async_computation.6 | async-start | bytes 1048576
  56.5 1.6 copy-start.4
  58.0 289.0 %reduce-scatter.5.cloned.1.call-start = ((), (), s32[]{:S(2)}) async-start(), calls=%async_computation.4 | async-start | bytes 557056 | tf_op jit(solution)/shard_map/reduce_scatter | solution.py:107
  61.8 536.2 %all-reduce.5.cloned.1.call-start = ((), (), s32[]{:S(2)}) async-start(), calls=%async_computation.3 | async-start | bytes 327680 | tf_op jit(solution)/shard_map/psum | solution.py:114
Sparse Core Ops, SparseCore 0:
  10.7 35.7 all-gather.1
  54.5 41.2 reduce-scatter.6
  98.7 155.1 all-reduce.6
  258.2 88.7 reduce-scatter.4
  349.8 248.1 all-reduce.4
where the time goes:
time: 609 us; the launch traced here: 606 us
  waiting for transfers between devices  562 us (92%)
  between operations  14.6 us (2%)
  matrix products  14.4 us (2%)
  local copies, waits for them, and re-layouts  8.87 us (1%)
  other arithmetic  6.13 us (1%)
    psum x1, waiting for transfers between devices, on_device(): cache_grad = lax.psum(ctx_share, 'head').astype(jnp.float32)  250 us
    unnamed x6, waiting for transfers between devices  157 us
    reduce_scatter x1, waiting for transfers between devices, on_device(): lax.psum_scatter(value_part, ('ctx', 'dp'), scatter_dimension=1, tiled=True)  91.8 us
    all_gather x1, waiting for transfers between devices, on_device(): key_block = lax.all_gather(own_rows, 'ctx', axis=0, tiled=True)  32.4 us
    reduce_scatter x1, waiting for transfers between devices, on_device(): lax.psum_scatter(grad_all.astype(jnp.bfloat16), 'ctx', scatter_dimension=...  31.3 us
  transfers between devices with their start and end apart: 5, of which 5 were waited for; matrix products, arithmetic and copies ran while one was open for 3% of the time, Pallas kernels for 0%

commit v1 on v0

v1 whole, which is shorter than its diff:
```python
import jax
import jax.numpy as jnp
from jax import lax
from jax.experimental import pallas as pl
from jax.experimental.pallas import tpu as pltpu
from jax.sharding import PartitionSpec as P

softmax_scale = 192.0 ** (-0.5)
MESH = pl.DeviceIdType.MESH
NY = 4
NZ = 16
f32 = jnp.float32
bf16 = jnp.bfloat16


class Copies:
    def __init__(self, send_sems, recv_sems):
        self.send_sems, self.recv_sems, self.made = send_sems, recv_sems, []

    def start(self, src, dst, device):
        at = len(self.made)
        copy = pltpu.make_async_remote_copy(
            src_ref=src,
            dst_ref=dst,
            send_sem=self.send_sems.at[at],
            recv_sem=self.recv_sems.at[at],
            device_id=device,
            device_id_type=MESH,
        )
        copy.start()
        self.made.append(copy)
        return copy

    def finish(self):
        for copy in self.made:
            copy.wait_send()


def entry_barrier(devices):
    barrier = pltpu.get_barrier_semaphore()
    for device in devices:
        pl.semaphore_signal(barrier, inc=1, device_id=device, device_id_type=MESH)
    pl.semaphore_wait(barrier, len(devices))


def total(*terms):
    terms = [term.astype(f32) for term in terms]
    result = terms[0]
    for term in terms[1:]:
        result = result + term
    return result


def gather_kernel(own_ref, all_ref, send_sems, recv_sems, own_sem):
    ctx = lax.axis_index("ctx")
    y, core = ctx // 2, ctx % 2

    def at(step, which):
        return {"ctx": lax.rem(y + step, NY) * 2 + which}

    def slot(step):
        return all_ref.at[lax.rem(y + step, NY) * 2 + core]

    ahead = 1 + 2 * core
    behind = 3 - 2 * core
    sibling = at(0, 1 - core)
    entry_barrier([sibling, at(1, core), at(3, core)])
    copies = Copies(send_sems, recv_sems)
    to_ahead = copies.start(own_ref, slot(0), at(ahead, core))
    to_behind = copies.start(own_ref, slot(0), at(behind, core))
    to_sibling = [copies.start(own_ref, slot(0), sibling)]
    keep = pltpu.make_async_copy(own_ref, slot(0), own_sem)
    keep.start()
    to_ahead.wait_recv()
    onward = copies.start(slot(behind), slot(behind), at(ahead, core))
    to_sibling.append(copies.start(slot(behind), slot(behind), sibling))
    to_behind.wait_recv()
    to_sibling.append(copies.start(slot(ahead), slot(ahead), sibling))
    onward.wait_recv()
    to_sibling.append(copies.start(slot(2), slot(2), sibling))
    for copy in to_sibling:
        copy.wait_recv()
    keep.wait()
    copies.finish()


def gather_rows(own_rows):
    rows, width = own_rows.shape
    return pl.pallas_call(
        gather_kernel,
        out_shape=jax.ShapeDtypeStruct((2 * NY, rows, width), bf16),
        in_specs=[pl.BlockSpec(memory_space=pltpu.VMEM)],
        out_specs=pl.BlockSpec(memory_space=pltpu.VMEM),
        scratch_shapes=[
            pltpu.SemaphoreType.DMA((7,)),
            pltpu.SemaphoreType.DMA((7,)),
            pltpu.SemaphoreType.DMA,
        ],
        compiler_params=pltpu.CompilerParams(collective_id=0, has_side_effects=True),
    )(own_rows)


def reduce_kernel(
    rows_ref, key_ref, value_ref,
    cache_ref, key_out, value_out,
    pair_rows, acc, ring_half, ring_in, block, z_in, piece, piece_in, final, done,
    pair_key, pair_value, key_acc, value_acc, key_half, value_half, key_in, value_in,
    key_sum, value_sum, key_far, value_far,
    send_sems, recv_sems,
):
    ctx = lax.axis_index("ctx")
    head = lax.axis_index("head")
    dp = lax.axis_index("dp")
    y, core = ctx // 2, ctx % 2
    z = lax.rem(head, NZ)
    x_lo = head // NZ
    chips = [lax.rem(y + step, NY) for step in range(NY)]
    sibling = {"ctx": y * 2 + 1 - core}
    up = {"ctx": chips[1] * 2 + core}
    down = {"ctx": chips[3] * 2 + core}
    z_at = [lax.rem(z + step, NZ) for step in range(NZ)]
    z_device = [{"head": x_lo * NZ + place} for place in z_at]
    x_pair = {"head": (1 - x_lo) * NZ + z}
    dp_pair = {"dp": 1 - dp}
    far_first = sorted(range(1, NZ), key=lambda step: -min(step, NZ - step))
    entry_barrier([sibling, up, down, x_pair, dp_pair] + [z_device[step] for step in far_first])
    copies = Copies(send_sems, recv_sems)

    pair = {}
    for step in (2, 1, 3, 0):
        pair[step] = copies.start(rows_ref.at[chips[step], 1 - core], pair_rows.at[step], sibling)
    pair_weights = [
        copies.start(key_ref.at[:, :, 1 - core], pair_key, sibling),
        copies.start(value_ref.at[:, :, 1 - core], pair_value, sibling),
    ]

    def join(step):
        pair[step].wait_recv()
        acc[step] = total(rows_ref[chips[step], core], pair_rows[step]).astype(bf16)

    join(2)
    up_far = copies.start(acc.at[2, 0], ring_half.at[0], up)
    down_far = copies.start(acc.at[2, 1], ring_half.at[1], down)
    join(1)
    up_own = copies.start(acc.at[1, 1], ring_in.at[0, 1], up)
    join(3)
    down_own = copies.start(acc.at[3, 0], ring_in.at[1, 0], down)
    join(0)
    up_far.wait_recv()
    acc[1, 0] = total(acc[1, 0], ring_half[0]).astype(bf16)
    up_both = copies.start(acc.at[1, 0], ring_in.at[0, 0], up)
    down_far.wait_recv()
    acc[3, 1] = total(acc[3, 1], ring_half[1]).astype(bf16)
    down_both = copies.start(acc.at[3, 1], ring_in.at[1, 1], down)

    for copy in pair_weights:
        copy.wait_recv()
    for step in range(NY):
        key_acc[step] = total(key_ref[:, chips[step], core], pair_key[:, chips[step]]).astype(bf16)
        value_acc[step] = total(value_ref[:, chips[step], core], pair_value[:, chips[step]]).astype(bf16)
    low, high = pl.ds(0, 2), pl.ds(2, 2)
    weights_far = [
        copies.start(key_acc.at[2, low], key_half.at[0], up),
        copies.start(value_acc.at[2, low], value_half.at[0], up),
        copies.start(key_acc.at[2, high], key_half.at[1], down),
        copies.start(value_acc.at[2, high], value_half.at[1], down),
    ]
    weights_in = [
        copies.start(key_acc.at[1, high], key_in.at[0, high], up),
        copies.start(value_acc.at[1, high], value_in.at[0, high], up),
        copies.start(key_acc.at[3, low], key_in.at[1, low], down),
        copies.start(value_acc.at[3, low], value_in.at[1, low], down),
    ]

    for copy in (up_own, down_own, up_both, down_both):
        copy.wait_recv()
    block[...] = total(acc[0], ring_in[0], ring_in[1]).astype(bf16).reshape(block.shape)
    scatter = [copies.start(block.at[z_at[step]], z_in.at[step], z_device[step]) for step in far_first]

    for copy in weights_far:
        copy.wait_recv()
    key_acc[1, low] = total(key_acc[1, low], key_half[0]).astype(bf16)
    value_acc[1, low] = total(value_acc[1, low], value_half[0]).astype(bf16)
    key_acc[3, high] = total(key_acc[3, high], key_half[1]).astype(bf16)
    value_acc[3, high] = total(value_acc[3, high], value_half[1]).astype(bf16)
    weights_in += [
        copies.start(key_acc.at[1, low], key_in.at[0, low], up),
        copies.start(value_acc.at[1, low], value_in.at[0, low], up),
        copies.start(key_acc.at[3, high], key_in.at[1, high], down),
        copies.start(value_acc.at[3, high], value_in.at[1, high], down),
    ]

    for copy in scatter:
        copy.wait_recv()
    piece[...] = total(block[z], *[z_in[step] for step in range(1, NZ)]).astype(bf16)
    across = copies.start(piece, piece_in, x_pair)

    for copy in weights_in:
        copy.wait_recv()
    key_sum[...] = total(key_acc[0], key_in[0], key_in[1]).astype(bf16)
    value_sum[...] = total(value_acc[0], value_in[0], value_in[1]).astype(bf16)
    weights_pair = [
        copies.start(key_sum.at[:, 1 - dp], key_far, dp_pair),
        copies.start(value_sum.at[:, 1 - dp], value_far, dp_pair),
    ]

    across.wait_recv()
    done[...] = total(piece[...], piece_in[...]).astype(bf16)
    final[z] = done[...]
    gather = [copies.start(done, final.at[z], z_device[step]) for step in far_first]

    for copy in weights_pair:
        copy.wait_recv()
    key_out[...] = total(key_sum[:, dp], key_far[...])
    value_out[...] = total(value_sum[:, dp], value_far[...])
    for copy in gather:
        copy.wait_recv()
    cache_ref[...] = final[...].astype(f32)
    copies.finish()


def reduce_all(grad_rows, key_part, value_part):
    width = grad_rows.shape[1]
    heads, nope, latent = key_part.shape
    values = value_part.shape[2]
    rows = grad_rows.reshape(NY, 2, 2, 64, width)
    keys = key_part.reshape(heads, NY, 2, 2, nope // 16, latent)
    vals = value_part.reshape(heads, NY, 2, 2, latent // 16, values)
    key_piece = (heads, 2, nope // 16, latent)
    value_piece = (heads, 2, latent // 16, values)
    half_key = (heads // 2,) + key_piece[1:]
    half_value = (heads // 2,) + value_piece[1:]
    n_copies = 4 + 2 + 6 + 8 + 4 + 15 + 1 + 2 + 15
    vmem = pl.BlockSpec(memory_space=pltpu.VMEM)
    cache, key_map, value_map = pl.pallas_call(
        reduce_kernel,
        out_shape=(
            jax.ShapeDtypeStruct((NZ, 8, width), f32),
            jax.ShapeDtypeStruct((heads, nope // 16, latent), f32),
            jax.ShapeDtypeStruct((heads, latent // 16, values), f32),
        ),
        in_specs=[vmem] * 3,
        out_specs=(vmem,) * 3,
        scratch_shapes=[
            pltpu.VMEM((NY, 2, 64, width), bf16),
            pltpu.VMEM((NY, 2, 64, width), bf16),
            pltpu.VMEM((2, 64, width), bf16),
            pltpu.VMEM((2, 2, 64, width), bf16),
            pltpu.VMEM((NZ, 8, width), bf16),
            pltpu.VMEM((NZ, 8, width), bf16),
            pltpu.VMEM((8, width), bf16),
            pltpu.VMEM((8, width), bf16),
            pltpu.VMEM((NZ, 8, width), bf16),
            pltpu.VMEM((8, width), bf16),
            pltpu.VMEM((heads, NY) + key_piece[1:], bf16),
            pltpu.VMEM((heads, NY) + value_piece[1:], bf16),
            pltpu.VMEM((NY,) + key_piece, bf16),
            pltpu.VMEM((NY,) + value_piece, bf16),
            pltpu.VMEM((2,) + half_key, bf16),
            pltpu.VMEM((2,) + half_value, bf16),
            pltpu.VMEM((2,) + key_piece, bf16),
            pltpu.VMEM((2,) + value_piece, bf16),
            pltpu.VMEM(key_piece, bf16),
            pltpu.VMEM(value_piece, bf16),
            pltpu.VMEM((heads, nope // 16, latent), bf16),
            pltpu.VMEM((heads, latent // 16, values), bf16),
            pltpu.SemaphoreType.DMA((n_copies,)),
            pltpu.SemaphoreType.DMA((n_copies,)),
        ],
        compiler_params=pltpu.CompilerParams(collective_id=1, has_side_effects=True),
    )(rows, keys, vals)
    return cache, key_map, value_map


def on_device(
    query_nope, query_rope, query_pos, latent_cache, block_table, key_up, value_up, grad_out
):
    latent_width = key_up.shape[2]
    page_rows = latent_cache.shape[2]
    row_width = latent_cache.shape[3]
    own_rows = latent_cache[0].reshape(-1, row_width)
    key_block = gather_rows(own_rows).reshape(-1, row_width)
    query_latent = jnp.einsum(
        "qhn,hnl->hql", query_nope[0], key_up, preferred_element_type=f32
    ).astype(bf16)
    query_rows = jnp.concatenate([query_latent, jnp.swapaxes(query_rope[0], 0, 1)], axis=2)
    grad_latent = jnp.einsum(
        "qhv,hlv->hql", grad_out[0], value_up, preferred_element_type=f32
    ).astype(bf16)
    query_position = query_pos[0]
    slot_table = block_table[0]

    row_index = jnp.arange(key_block.shape[0], dtype=jnp.int32)
    logical = jnp.sum(
        jnp.where(
            slot_table[None, :] == (row_index // page_rows)[:, None],
            jnp.arange(slot_table.shape[0], dtype=jnp.int32)[None, :],
            0,
        ),
        axis=1,
    )
    position = logical * page_rows + row_index % page_rows
    scores = (
        jnp.einsum("hqc,kc->hqk", query_rows, key_block, preferred_element_type=f32)
        * softmax_scale
    )
    visible = position[None, None, :] <= query_position[None, :, None]
    scores = jnp.where(visible, scores, -jnp.inf)
    grad_probs = jnp.einsum(
        "hql,kl->hqk", grad_latent, key_block[:, :latent_width], preferred_element_type=f32
    )
    weights = jnp.exp(scores - jnp.max(scores, axis=2, keepdims=True))
    denominator = jnp.sum(weights, axis=2, keepdims=True)
    row_delta = jnp.sum(weights * grad_probs, axis=2, keepdims=True) / denominator
    attn_probs = weights / denominator
    probs_b = attn_probs.astype(bf16)
    grad_scores = (attn_probs * (grad_probs - row_delta) * softmax_scale).astype(bf16)
    grad_rows = jnp.einsum("hqk,hqc->kc", grad_scores, query_rows, preferred_element_type=f32)
    grad_values = jnp.einsum("hqk,hql->kl", probs_b, grad_latent, preferred_element_type=f32)
    grad_rows = grad_rows + jnp.pad(grad_values, ((0, 0), (0, row_width - latent_width)))
    grad_query = jnp.einsum("hqk,kc->hqc", grad_scores, key_block, preferred_element_type=f32)
    attn_out = jnp.einsum(
        "hqk,kl->hql", probs_b, key_block[:, :latent_width], preferred_element_type=f32
    ).astype(bf16)
    grad_rope = jnp.swapaxes(grad_query[..., latent_width:], 0, 1)[None]
    grad_qlatent = grad_query[..., :latent_width].astype(bf16)
    grad_nope = jnp.einsum("hql,hnl->qhn", grad_qlatent, key_up, preferred_element_type=f32)[None]
    key_part = jnp.einsum(
        "qhn,hql->hnl", query_nope[0], grad_qlatent, preferred_element_type=f32
    ).astype(bf16)
    value_part = jnp.einsum(
        "hql,qhv->hlv", attn_out, grad_out[0], preferred_element_type=f32
    ).astype(bf16)
    cache_grad, grad_key_map, grad_value_map = reduce_all(
        grad_rows.astype(bf16), key_part, value_part
    )
    return (
        grad_nope,
        grad_rope,
        cache_grad.reshape(latent_cache.shape),
        grad_key_map,
        grad_value_map,
    )


def solution(mesh):
    placed = (
        P("dp", "ctx", "head", None),
        P("dp", "ctx", "head", None),
        P("dp", "ctx"),
        P("dp", "ctx", None, None),
        P("dp", None),
        P("head", None, None),
        P("head", None, None),
        P("dp", "ctx", "head", None),
    )
    return jax.shard_map(
        on_device,
        mesh=mesh,
        in_specs=placed,
        out_specs=(
            P("dp", "ctx", "head", None),
            P("dp", "ctx", "head", None),
            P("dp", "ctx", None, None),
            P("head", ("ctx", "dp"), None),
            P("head", ("ctx", "dp"), None),
        ),
        check_vma=False,
    )
```

time: 609 us -> 96.9 us (0.16)
  waiting for transfers between devices: 562 us -> 0 us
  Pallas kernels: 0 us -> 62.1 us
  between operations: 14.6 us -> 0.78 us
    psum x1 -> x0, waiting for transfers between devices: 250 us -> none  [on_device(): cache_grad = lax.psum(ctx_share, 'head').astype(jnp.float32)]
    unnamed x6 -> x0, waiting for transfers between devices: 157 us -> none
    reduce_scatter x2 -> x0, waiting for transfers between devices: 123 us -> none  [the longest x1 91.8 us: on_device(): lax.psum_scatter(value_part, ('ctx', 'dp'), scatter_dimension=1, tiled=True)]
    pallas_call x0 -> x2, Pallas kernels: none -> 62.1 us  [the longest x1 46 us: reduce_all(): pl.pallas_call(reduce_kernel, out_shape=(jax.ShapeDtypeStruct((NZ, 8, wid...]
    all_gather x1 -> x0, waiting for transfers between devices: 32.4 us -> none  [on_device(): key_block = lax.all_gather(own_rows, 'ctx', axis=0, tiled=True)]
  transfers between devices with their start and end apart: 5 -> 0, of which waited for: 5 -> 0; matrix products, arithmetic and copies ran while one was open for 3% -> 0% of each run, Pallas kernels for 0% -> 0%
where the time goes in v1:
time: 96.9 us; the launch traced here: 95.7 us
  Pallas kernels  62.1 us (64%)
  matrix products  18.1 us (19%)
  local copies, waits for them, and re-layouts  10.1 us (10%)
  other arithmetic  4.66 us (5%)
    pallas_call x1, Pallas kernels, reduce_all(): pl.pallas_call(reduce_kernel, out_shape=(jax.ShapeDtypeStruct((NZ, 8, wid...  46 us
    pallas_call x1, Pallas kernels, gather_rows(): pl.pallas_call(gather_kernel, out_shape=jax.ShapeDtypeStruct((2 * NY, row...  16.1 us
    unnamed x17, local copies, waits for them, and re-layouts  6.96 us
    sub x1, matrix products, on_device(): weights = jnp.exp(scores - jnp.max(scores, axis=2, keepdims=True))  4.28 us
    dot_general x1, matrix products, on_device(): jnp.einsum('hql,qhv->hlv', attn_out, grad_out[0], preferred_element_type=...  3.7 us
    convert_element_type x1, other arithmetic, on_device(): (attn_probs * (grad_probs - row_delta) * softmax_scale).astype(bf16)  3.03 us
    dot_general x1, matrix products, on_device(): jnp.einsum('hqk,hql->kl', probs_b, grad_latent, preferred_element_type=f32)  2.47 us
    dot_general x1, matrix products, on_device(): jnp.einsum('hql,kl->hqk', grad_latent, key_block[:, :latent_width], prefe...  2.13 us

profile of v1, /device:TPU:6, one launch (start us, length us, event | category | flops | bytes accessed | tf_op | source)
XLA Modules:
  0.0 95.7 jit_solution(2174157231763366472)
XLA Ops:
  0.6 0.0 copy-start
  0.6 0.0 copy-start.4
  0.7 0.8 select_reduce_fusion
  1.5 0.8 broadcast_compare_fusion
  2.3 1.0 %copy.38 = bf16[128,4,128]{0,2,1:T(8,128)(2,1)S(1)} copy(bf16[128,4,128]{2,1,0:T(4,128)(2,1)} %bitcast.61) | data formatting | bytes 262144 | tf_op jit(solution)/shard_map/squeeze | solution.py:284
  3.4 1.0 %copy.28 = bf16[1,128,4,64]{3,1,2,0:T(8,128)(2,1)S(1)} copy(bf16[1,128,4,64]{1,3,2,0:T(8,128)(2,1)} %param.9) | data formatting | bytes 131072 | tf_op args[1]
  4.3 0.0 copy-done
  4.3 0.3 convolution_convert_fusion.3
  4.7 0.0 copy-done.4
  4.7 2.0 %convolution_convert_fusion.2 = bf16[4,128,512]{2,1,0:T(8,128)(2,1)} fusion(bf16[4,512,128]{2,1,0:T(8,128)(2,1)S(1)} %copy-done.4, bf16[128,4,128]{2,1,0:T(4,128)(2,1)} %bitcast.59), kind=kOutput, calls=%fused_computation.11 | convolution fusion | flops 67371008 | bytes 1179648 | tf_op jit(solution)/shard_map/qhv,hlv->hql/dot_general | solution.py:287
  6.7 16.1 %shard_map.119 = bf16[8,128,576]{2,1,0:T(8,128)(2,1)} custom-call(bf16[128,576]{1,0:T(8,128)(2,1)} %bitcast.58), custom_call_target="tpu_custom_call" | custom-call | tf_op jit(solution)/shard_map/pallas_call | solution.py:89
  22.8 2.1 %fusion.7 = f32[4,128,1024]{2,1,0:T(8,128)S(1)} fusion(bf16[4,128,512]{2,1,0:T(8,128)(2,1)} %convolution_convert_fusion.2, bf16[1024,576]{1,0:T(8,128)(2,1)} %bitcast.49), kind=kOutput, calls=%fused_computation.22 | convolution fusion | flops 536870912 | bytes 3670016 | tf_op jit(solution)/shard_map/hql,kl->hqk/dot_general | solution.py:309
  24.9 4.3 %fusion.28 = (f32[4,128]{1,0:T(4,128)S(1)}, f32[4,128]{1,0:T(4,128)S(1)}, f32[4,128,1024]{2,1,0:T(8,128)}) fusion(f32[4,128,1024]{2,1,0:T(8,128)S(1)} %fusion.7, pred[128,1024]{1,0:T(8,128)(4,1)S(1)} %broadcast_compare_fusion, bf16[1024,576,1]{1,0,2:T(8,128)(2,1)} %bitcast.50, bf16[4,128,64]{2,1,0:T(8,128)(2,1)S(1)} %bitcast.54, ...), kind=kOutput, calls=%fused_computation.47 | convolution fusion | flops 608305664 | bytes 6098944 | tf_op jit(solution)/shard_map/sub | solution.py:312
  29.2 0.0 copy-start.5
  29.2 3.0 %multiply_convert_fusion = bf16[4,128,1024]{2,1,0:T(8,128)(2,1)} fusion(f32[4,128,1024]{2,1,0:T(8,128)S(1)} %fusion.7, f32[4,128]{1,0:T(4,128)S(1)} %div.28, f32[4,128,1024]{2,1,0:T(8,128)} %get-tuple-element.23, f32[4,128]{1,0:T(4,128)S(1)} %get-tuple-element.21), kind=kLoop, calls=%fused_computation.3 | loop fusion | flops 2621440 | bytes 5246976 | tf_op jit(solution)/shard_map/convert_element_type | solution.py:317
  32.2 0.0 copy-done.5
  32.2 0.0 copy-start.3
  32.2 3.7 %convolution_convert_fusion = bf16[4,512,128]{2,1,0:T(8,128)(2,1)} fusion(bf16[1024,576]{1,0:T(8,128)(2,1)} %bitcast.51, bf16[128,4,128]{2,1,0:T(4,128)(2,1)S(1)} %bitcast.60, f32[4,128,1024]{2,1,0:T(8,128)} %get-tuple-element.23, f32[4,128]{1,0:T(4,128)S(1)} %get-tuple-element.21), kind=kOutput, calls=%fused_computation.9 | convolution fusion | flops 605552640 | bytes 3803136 | tf_op jit(solution)/shard_map/hql,qhv->hlv/dot_general | solution.py:331
  35.9 0.0 copy-done.3
  35.9 0.0 copy-start.2
  35.9 2.5 %convolution_bitcast_fusion = f32[1024,512]{0,1:T(8,128)S(1)} fusion(bf16[4,128,512]{2,1,0:T(8,128)(2,1)S(1)} %copy-done.3, f32[4,128,1024]{2,1,0:T(8,128)} %get-tuple-element.23, f32[4,128]{1,0:T(4,128)S(1)} %get-tuple-element.21), kind=kOutput, calls=%fused_computation.8 | convolution fusion | flops 537919488 | bytes 4720640 | tf_op jit(solution)/shard_map/hqk,hql->kl/dot_general | solution.py:319
  38.4 0.0 copy-done.2
  38.4 0.0 copy-start.1
  38.4 0.9 fusion.1
  39.3 0.4 copy-done.1
  39.7 0.8 fusion.29
  40.6 0.7 slice_bitcast_fusion.4
  41.2 1.4 %copy.36 = bf16[1024,576]{1,0:T(8,128)(2,1)} copy(bf16[1024,576]{0,1:T(8,128)(2,1)S(1)} %fusion.1) | data formatting | bytes 2359296 | tf_op jit(solution)/shard_map/convert_element_type | solution.py:335
  42.7 0.3 convolution_bitcast_fusion.1
  43.0 1.1 %convolution_convert_fusion.1 = bf16[4,512,128]{1,2,0:T(8,128)(2,1)} fusion(bf16[128,4,128]{0,2,1:T(8,128)(2,1)S(1)} %copy.38, f32[4,128,576]{1,2,0:T(8,128)S(1)} %fusion.29), kind=kOutput, calls=%fused_computation.10 | convolution fusion | flops 67371008 | bytes 1179648 | tf_op jit(solution)/shard_map/qhn,hql->hnl/dot_general | solution.py:328
  44.1 46.0 %shard_map.120 = (f32[16,8,576]{2,1,0:T(8,128)}, f32[4,8,512]{2,1,0:T(8,128)}, f32[4,32,128]{2,1,0:T(8,128)}) custom-call(bf16[4,2,2,64,576]{4,3,2,1,0:T(8,128)(2,1)} %bitcast.48, bf16[4,4,2,2,8,512]{5,4,3,2,1,0:T(8,128)(2,1)} %bitcast.53, bf16[4,4,2,2,32,128]{5,4,3,2,1,0:T(8,128)(2,1)} %bitcast.56), custom_call_target="tpu_custom_call" | custom-call | tf_op jit(solution)/shard_map/pallas_call | solution.py:235
  90.2 0.9 copy.40
  91.1 1.7 %copy.57 = f32[1,2,64,576]{3,2,1,0:T(8,128)} copy(f32[1,2,64,576]{3,2,1,0:T(8,128)} %bitcast.57) | data formatting | bytes 589824
  92.8 1.5 %copy.58 = f32[4,8,512]{2,1,0:T(8,128)} copy(f32[4,8,512]{2,1,0:T(8,128)} %get-tuple-element.32) | data formatting | bytes 131072
  94.3 1.5 %copy.59 = f32[4,32,128]{2,1,0:T(8,128)} copy(f32[4,32,128]{2,1,0:T(8,128)} %get-tuple-element.33) | data formatting | bytes 131072
  (3 shorter events, 0.0 us)
Async XLA Ops:
  0.6 3.7 %copy-start = (bf16[4,128,512]{2,1,0:T(8,128)(2,1)S(1)}, bf16[4,128,512]{2,1,0:T(8,128)(2,1)}, u32[]{:S(2)}) copy-start(bf16[4,128,512]{2,1,0:T(8,128)(2,1)} %param.13) | copy-start | bytes 1572868
  0.6 4.0 %copy-start.4 = (bf16[4,512,128]{2,1,0:T(8,128)(2,1)S(1)}, bf16[4,512,128]{2,1,0:T(8,128)(2,1)}, u32[]{:S(2)}) copy-start(bf16[4,512,128]{2,1,0:T(8,128)(2,1)} %param.14) | copy-start | bytes 1572868
  29.2 3.0 %copy-start.5 = (bf16[1,128,4,128]{3,2,1,0:T(4,128)(2,1)S(1)}, bf16[1,128,4,128]{3,2,1,0:T(4,128)(2,1)}, u32[]{:S(2)}) copy-start(bf16[1,128,4,128]{3,2,1,0:T(4,128)(2,1)} %param.15) | copy-start | bytes 393220
  32.2 3.7 %copy-start.3 = (bf16[4,128,512]{2,1,0:T(8,128)(2,1)S(1)}, bf16[4,128,512]{2,1,0:T(8,128)(2,1)}, u32[]{:S(2)}) copy-start(bf16[4,128,512]{2,1,0:T(8,128)(2,1)} %convolution_convert_fusion.2) | copy-start | bytes 1572868
  35.9 2.5 %copy-start.2 = (bf16[4,128,1024]{2,1,0:T(8,128)(2,1)S(1)}, bf16[4,128,1024]{2,1,0:T(8,128)(2,1)}, u32[]{:S(2)}) copy-start(bf16[4,128,1024]{2,1,0:T(8,128)(2,1)} %multiply_convert_fusion) | copy-start | bytes 3145732
  38.4 1.3 %copy-start.1 = (bf16[8,128,576]{2,1,0:T(8,128)(2,1)S(1)}, bf16[8,128,576]{2,1,0:T(8,128)(2,1)}, u32[]{:S(2)}) copy-start(bf16[8,128,576]{2,1,0:T(8,128)(2,1)} %shard_map.119) | copy-start | bytes 3538948

commit v2 on v1

v2 whole, which is shorter than its diff:
```python
import jax
import jax.numpy as jnp
from jax import lax
from jax.experimental import pallas as pl
from jax.experimental.pallas import tpu as pltpu
from jax.sharding import PartitionSpec as P

softmax_scale = 192.0 ** (-0.5)
MESH = pl.DeviceIdType.MESH
NY = 4
NZ = 16
HEADS = 4
f32 = jnp.float32
bf16 = jnp.bfloat16


class Copies:
    def __init__(self, send_sems, recv_sems):
        self.send_sems, self.recv_sems, self.made = send_sems, recv_sems, []

    def start(self, src, dst, device):
        at = len(self.made)
        copy = pltpu.make_async_remote_copy(
            src_ref=src,
            dst_ref=dst,
            send_sem=self.send_sems.at[at],
            recv_sem=self.recv_sems.at[at],
            device_id=device,
            device_id_type=MESH,
        )
        copy.start()
        self.made.append(copy)
        return copy

    def finish(self):
        for copy in self.made:
            copy.wait_send()


def entry_barrier(devices):
    barrier = pltpu.get_barrier_semaphore()
    for device in devices:
        pl.semaphore_signal(barrier, inc=1, device_id=device, device_id_type=MESH)
    pl.semaphore_wait(barrier, len(devices))


def total(*terms):
    terms = [term.astype(f32) for term in terms]
    result = terms[0]
    for term in terms[1:]:
        result = result + term
    return result


def dot(a, b, a_dim, b_dim):
    return lax.dot_general(a, b, (((a_dim,), (b_dim,)), ((), ())), preferred_element_type=f32)


def iota(shape, dim):
    return lax.broadcasted_iota(jnp.int32, shape, dim)


def one_head(values, head):
    return jnp.where(lax.rem(iota(values.shape, 0), HEADS) == head, values.astype(f32), 0.0).astype(bf16)


def gather_kernel(
    own_ref, nope_ref, grad_ref, rope_ref, key_up_ref, value_up_ref,
    all_ref, query_ref, latent_ref,
    send_sems, recv_sems, own_sem,
):
    ctx = lax.axis_index("ctx")
    y, core = ctx // 2, ctx % 2

    def at(step, which):
        return {"ctx": lax.rem(y + step, NY) * 2 + which}

    def slot(step):
        return all_ref.at[lax.rem(y + step, NY) * 2 + core]

    ahead = 1 + 2 * core
    behind = 3 - 2 * core
    sibling = at(0, 1 - core)
    entry_barrier([sibling, at(1, core), at(3, core)])
    copies = Copies(send_sems, recv_sems)
    to_ahead = copies.start(own_ref, slot(0), at(ahead, core))
    to_behind = copies.start(own_ref, slot(0), at(behind, core))
    to_sibling = [copies.start(own_ref, slot(0), sibling)]
    keep = pltpu.make_async_copy(own_ref, slot(0), own_sem)
    keep.start()

    latent = key_up_ref.shape[2]
    rope = rope_ref.shape[0] // HEADS

    @pl.loop(0, nope_ref.shape[0] // 128)
    def _(step):
        rows = pl.ds(step * 128, 128)
        nope, grad = nope_ref[rows, :], grad_ref[rows, :]
        spread = jnp.concatenate([one_head(nope, head) for head in range(HEADS)], axis=1)
        up = key_up_ref[...].reshape(spread.shape[1], latent)
        query_ref[rows, :latent] = dot(spread, up, 1, 0).astype(bf16)
        latent_ref[rows, :] = total(
            *[dot(one_head(grad, head), value_up_ref[head], 1, 1) for head in range(HEADS)]
        ).astype(bf16)
        query = (iota((128, 128), 0) + step * 128) // HEADS
        pick = (iota((128, 128), 1) == query).astype(f32).astype(bf16)
        every = dot(pick, rope_ref[...], 1, 1)
        shape = every.shape
        mine = iota(shape, 1) // rope == lax.rem(iota(shape, 0), HEADS)
        fold = (lax.rem(iota((shape[1], rope), 0), rope) == iota((shape[1], rope), 1)).astype(f32).astype(bf16)
        query_ref[rows, latent:] = dot(jnp.where(mine, every, 0.0).astype(bf16), fold, 1, 0).astype(bf16)

    to_ahead.wait_recv()
    onward = copies.start(slot(behind), slot(behind), at(ahead, core))
    to_sibling.append(copies.start(slot(behind), slot(behind), sibling))
    to_behind.wait_recv()
    to_sibling.append(copies.start(slot(ahead), slot(ahead), sibling))
    onward.wait_recv()
    to_sibling.append(copies.start(slot(2), slot(2), sibling))
    for copy in to_sibling:
        copy.wait_recv()
    keep.wait()
    copies.finish()


def gather_and_project(own_rows, nope, grad, rope, key_up, value_up):
    rows, width = own_rows.shape
    latent = key_up.shape[2]
    vmem = pl.BlockSpec(memory_space=pltpu.VMEM)
    return pl.pallas_call(
        gather_kernel,
        out_shape=(
            jax.ShapeDtypeStruct((2 * NY, rows, width), bf16),
            jax.ShapeDtypeStruct((nope.shape[0], width), bf16),
            jax.ShapeDtypeStruct((nope.shape[0], latent), bf16),
        ),
        in_specs=[vmem] * 6,
        out_specs=(vmem,) * 3,
        scratch_shapes=[
            pltpu.SemaphoreType.DMA((7,)),
            pltpu.SemaphoreType.DMA((7,)),
            pltpu.SemaphoreType.DMA,
        ],
        compiler_params=pltpu.CompilerParams(collective_id=0, has_side_effects=True),
    )(own_rows, nope, grad, rope, key_up, value_up)


def main_kernel(
    table_ref, pos_ref, keys_ref, query_ref, latent_ref, nope_ref, grad_ref, key_up_ref,
    nope_out, rope_out, cache_ref, key_out, value_out,
    key_pos, scores, grad_probs, score_t, prob_t, query_grad, rope_parts, out_t,
    rows_out, pair_rows, acc, ring_half, ring_in, block, z_in, piece, piece_in, final, done,
    key_part, value_part,
    pair_key, pair_value, key_acc, value_acc, key_half, value_half, key_in, value_in,
    key_sum, value_sum, key_far, value_far,
    send_sems, recv_sems,
):
    ctx = lax.axis_index("ctx")
    head = lax.axis_index("head")
    dp = lax.axis_index("dp")
    y, core = ctx // 2, ctx % 2
    z = lax.rem(head, NZ)
    x_lo = head // NZ
    chips = [lax.rem(y + step, NY) for step in range(NY)]
    sibling = {"ctx": y * 2 + 1 - core}
    up = {"ctx": chips[1] * 2 + core}
    down = {"ctx": chips[3] * 2 + core}
    z_at = [lax.rem(z + step, NZ) for step in range(NZ)]
    z_device = [{"head": x_lo * NZ + place} for place in z_at]
    x_pair = {"head": (1 - x_lo) * NZ + z}
    dp_pair = {"dp": 1 - dp}
    far_first = sorted(range(1, NZ), key=lambda step: -min(step, NZ - step))
    friends = [z_device[step] for step in far_first] + [x_pair, dp_pair, up, down, sibling]
    barrier = pltpu.get_barrier_semaphore()
    for device in friends:
        pl.semaphore_signal(barrier, inc=1, device_id=device, device_id_type=MESH)

    blocks = table_ref.shape[1]
    page = keys_ref.shape[0] // blocks
    lanes = key_pos.shape[1]
    for slot in range(blocks):
        start = sum(jnp.where(table_ref[0, at] == slot, at * page, 0) for at in range(blocks))
        key_pos[slot * page:(slot + 1) * page, :] = (iota((page, lanes), 0) + start).astype(f32)
    count = query_ref.shape[0]
    spread = (iota((count // HEADS, count), 0) == iota((count // HEADS, count), 1) // HEADS).astype(f32).astype(bf16)
    pos = jnp.broadcast_to(pos_ref[...], (8, count // HEADS))
    pos_high, pos_low = pos // 32, lax.rem(pos, 32)
    query_pos = (
        dot(pos_high.astype(f32).astype(bf16), spread, 1, 0) * 32.0
        + dot(pos_low.astype(f32).astype(bf16), spread, 1, 0)
    )
    latent = latent_ref.shape[1]
    width = keys_ref.shape[1]
    n_keys = keys_ref.shape[0]
    chunk = 256
    n_chunks = n_keys // chunk

    for part in range(count // lanes):
        mine = slice(part * lanes, (part + 1) * lanes)
        at_pos = query_pos[0:1, mine]

        def score_step(step, row_max):
            rows = pl.ds(step * chunk, chunk)
            raw = dot(keys_ref[rows, :], query_ref[mine, :], 1, 1) * softmax_scale
            raw = jnp.where(key_pos[rows, :] <= at_pos, raw, -jnp.inf)
            scores[rows, :] = raw
            grad_probs[rows, :] = dot(keys_ref[rows, :latent], latent_ref[mine, :], 1, 1)
            return jnp.maximum(row_max, jnp.max(raw, axis=0, keepdims=True))

        row_max = lax.fori_loop(0, n_chunks, score_step, jnp.full((1, lanes), -jnp.inf, f32))

        def weight_step(step, sums):
            rows = pl.ds(step * chunk, chunk)
            weights = jnp.exp(scores[rows, :] - row_max)
            scores[rows, :] = weights
            return (
                sums[0] + jnp.sum(weights, axis=0, keepdims=True),
                sums[1] + jnp.sum(weights * grad_probs[rows, :], axis=0, keepdims=True),
            )

        zero = jnp.zeros((1, lanes), f32)
        denominator, weighted = lax.fori_loop(0, n_chunks, weight_step, (zero, zero))
        scale = 1.0 / denominator
        row_delta = weighted * scale

        def grad_step(step, carry):
            rows = pl.ds(step * chunk, chunk)
            probs = scores[rows, :] * scale
            prob_t[rows, mine] = probs.astype(bf16)
            score_t[rows, mine] = (probs * (grad_probs[rows, :] - row_delta) * softmax_scale).astype(bf16)
            return carry

        lax.fori_loop(0, n_chunks, grad_step, 0)

    pl.semaphore_wait(barrier, len(friends))
    copies = Copies(send_sems, recv_sems)

    def grad_rows(chip, which):
        rows = pl.ds(pl.multiple_of((chip * 2 + which) * 128, 128), 128)
        by_score = dot(score_t[rows, :], query_ref[...], 1, 0)
        by_prob = dot(prob_t[rows, :], latent_ref[...], 1, 0)
        return by_score[:, :latent] + by_prob, by_score[:, latent:]

    pair = {}
    for step in (2, 1, 3, 0):
        low, high = grad_rows(chips[step], 1 - core)
        rows_out[step, :, :, :latent] = low.astype(bf16).reshape(2, 64, latent)
        rows_out[step, :, :, latent:] = high.astype(bf16).reshape(2, 64, width - latent)
        pair[step] = copies.start(rows_out.at[step], pair_rows.at[step], sibling)

    def join(step):
        low, high = grad_rows(chips[step], core)
        pair[step].wait_recv()
        acc[step, :, :, :latent] = total(low.reshape(2, 64, latent), pair_rows[step, :, :, :latent]).astype(bf16)
        acc[step, :, :, latent:] = total(
            high.reshape(2, 64, width - latent), pair_rows[step, :, :, latent:]
        ).astype(bf16)

    join(2)
    up_far = copies.start(acc.at[2, 0], ring_half.at[0], up)
    down_far = copies.start(acc.at[2, 1], ring_half.at[1], down)
    join(1)
    up_own = copies.start(acc.at[1, 1], ring_in.at[0, 1], up)
    join(3)
    down_own = copies.start(acc.at[3, 0], ring_in.at[1, 0], down)
    join(0)
    up_far.wait_recv()
    acc[1, 0] = total(acc[1, 0], ring_half[0]).astype(bf16)
    up_both = copies.start(acc.at[1, 0], ring_in.at[0, 0], up)
    down_far.wait_recv()
    acc[3, 1] = total(acc[3, 1], ring_half[1]).astype(bf16)
    down_both = copies.start(acc.at[3, 1], ring_in.at[1, 1], down)

    @pl.loop(0, count // 128)
    def _(step):
        lane = pl.ds(pl.multiple_of(step * 128, 128), 128)
        grad = dot(score_t[:, lane], keys_ref[...], 0, 0)
        query_grad[lane, :] = grad[:, :latent].astype(bf16)
        rope_high = grad[:, latent:].astype(bf16)
        rope_parts[lane, :width - latent] = rope_high
        rope_parts[lane, width - latent:] = (grad[:, latent:] - rope_high.astype(f32)).astype(bf16)

    for copy in (up_own, down_own, up_both, down_both):
        copy.wait_recv()
    block[...] = total(acc[0], ring_in[0], ring_in[1]).astype(bf16).reshape(block.shape)
    scatter = [copies.start(block.at[z_at[step]], z_in.at[step], z_device[step]) for step in far_first]

    @pl.loop(0, HEADS)
    def _(at):
        part = dot(one_head(nope_ref[...], at), query_grad[...], 0, 0)
        key_part[at] = part.astype(bf16).reshape(key_part.shape[1:])

    pair_weights = [copies.start(key_part.at[:, :, 1 - core], pair_key, sibling)]

    @pl.loop(0, latent // 128)
    def _(step):
        lane = pl.ds(pl.multiple_of(step * 128, 128), 128)
        out_t[lane, :] = dot(keys_ref[:, lane], prob_t[...], 0, 0).astype(bf16)

    @pl.loop(0, HEADS)
    def _(at):
        part = dot(out_t[...], one_head(grad_ref[...], at), 1, 0)
        value_part[at] = part.astype(bf16).reshape(value_part.shape[1:])

    pair_weights.append(copies.start(value_part.at[:, :, 1 - core], pair_value, sibling))

    @pl.loop(0, count // 128)
    def _(step):
        rows = pl.ds(step * 128, 128)
        every = dot(query_grad[rows, :], key_up_ref[...].reshape(-1, latent), 1, 1)
        n = nope_out.shape[1]
        which = lax.rem(iota((128, n), 0), HEADS)
        nope_out[rows, :] = total(
            *[jnp.where(which == at, every[:, at * n:(at + 1) * n], 0.0) for at in range(HEADS)]
        )

    rope = width - latent
    queries = count // HEADS
    for at in range(HEADS):
        order = (iota((count, queries), 0) == iota((count, queries), 1) * HEADS + at).astype(f32).astype(bf16)
        turned = dot(rope_parts[...], order, 0, 0)
        rope_out[at * rope:(at + 1) * rope, :] = turned[:rope] + turned[rope:]

    for copy in pair_weights:
        copy.wait_recv()
    for step in range(NY):
        key_acc[step] = total(key_part[:, chips[step], core], pair_key[:, chips[step]]).astype(bf16)
        value_acc[step] = total(value_part[:, chips[step], core], pair_value[:, chips[step]]).astype(bf16)
    low, high = pl.ds(0, 2), pl.ds(2, 2)
    weights_far = [
        copies.start(key_acc.at[2, low], key_half.at[0], up),
        copies.start(value_acc.at[2, low], value_half.at[0], up),
        copies.start(key_acc.at[2, high], key_half.at[1], down),
        copies.start(value_acc.at[2, high], value_half.at[1], down),
    ]
    weights_in = [
        copies.start(key_acc.at[1, high], key_in.at[0, high], up),
        copies.start(value_acc.at[1, high], value_in.at[0, high], up),
        copies.start(key_acc.at[3, low], key_in.at[1, low], down),
        copies.start(value_acc.at[3, low], value_in.at[1, low], down),
    ]
    for copy in weights_far:
        copy.wait_recv()
    key_acc[1, low] = total(key_acc[1, low], key_half[0]).astype(bf16)
    value_acc[1, low] = total(value_acc[1, low], value_half[0]).astype(bf16)
    key_acc[3, high] = total(key_acc[3, high], key_half[1]).astype(bf16)
    value_acc[3, high] = total(value_acc[3, high], value_half[1]).astype(bf16)
    weights_in += [
        copies.start(key_acc.at[1, low], key_in.at[0, low], up),
        copies.start(value_acc.at[1, low], value_in.at[0, low], up),
        copies.start(key_acc.at[3, high], key_in.at[1, high], down),
        copies.start(value_acc.at[3, high], value_in.at[1, high], down),
    ]

    for copy in scatter:
        copy.wait_recv()
    piece[...] = total(block[z], *[z_in[step] for step in range(1, NZ)]).astype(bf16)
    across = copies.start(piece, piece_in, x_pair)
    across.wait_recv()
    done[...] = total(piece[...], piece_in[...]).astype(bf16)
    final[z] = done[...]
    gather = [copies.start(done, final.at[z], z_device[step]) for step in far_first]

    for copy in weights_in:
        copy.wait_recv()
    key_sum[...] = total(key_acc[0], key_in[0], key_in[1]).astype(bf16)
    value_sum[...] = total(value_acc[0], value_in[0], value_in[1]).astype(bf16)
    weights_pair = [
        copies.start(key_sum.at[:, 1 - dp], key_far, dp_pair),
        copies.start(value_sum.at[:, 1 - dp], value_far, dp_pair),
    ]
    for copy in weights_pair:
        copy.wait_recv()
    key_out[...] = total(key_sum[:, dp], key_far[...])
    value_out[...] = total(value_sum[:, dp], value_far[...])
    for copy in gather:
        copy.wait_recv()
    cache_ref[...] = final[...].astype(f32)
    copies.finish()


def attend_and_reduce(table, pos, keys, query_rows, grad_latent, nope, grad, key_up):
    n_keys, width = keys.shape
    count, n_nope = nope.shape
    heads, _, latent = key_up.shape
    values = grad.shape[1]
    key_piece = (heads, 2, n_nope // 16, latent)
    value_piece = (heads, 2, latent // 16, values)
    half_key = (heads // 2,) + key_piece[1:]
    half_value = (heads // 2,) + value_piece[1:]
    n_copies = 4 + 2 + 6 + 8 + 4 + 15 + 1 + 2 + 15
    vmem = pl.BlockSpec(memory_space=pltpu.VMEM)
    return pl.pallas_call(
        main_kernel,
        out_shape=(
            jax.ShapeDtypeStruct((count, n_nope), f32),
            jax.ShapeDtypeStruct((heads * (width - latent), count // heads), f32),
            jax.ShapeDtypeStruct((NZ, 8, width), f32),
            jax.ShapeDtypeStruct((heads, n_nope // 16, latent), f32),
            jax.ShapeDtypeStruct((heads, latent // 16, values), f32),
        ),
        in_specs=[pl.BlockSpec(memory_space=pltpu.SMEM)] + [vmem] * 7,
        out_specs=(vmem,) * 5,
        scratch_shapes=[
            pltpu.VMEM((n_keys, 256), f32),
            pltpu.VMEM((n_keys, 256), f32),
            pltpu.VMEM((n_keys, 256), f32),
            pltpu.VMEM((n_keys, count), bf16),
            pltpu.VMEM((n_keys, count), bf16),
            pltpu.VMEM((count, latent), bf16),
            pltpu.VMEM((count, 2 * (width - latent)), bf16),
            pltpu.VMEM((latent, count), bf16),
            pltpu.VMEM((NY, 2, 64, width), bf16),
            pltpu.VMEM((NY, 2, 64, width), bf16),
            pltpu.VMEM((NY, 2, 64, width), bf16),
            pltpu.VMEM((2, 64, width), bf16),
            pltpu.VMEM((2, 2, 64, width), bf16),
            pltpu.VMEM((NZ, 8, width), bf16),
            pltpu.VMEM((NZ, 8, width), bf16),
            pltpu.VMEM((8, width), bf16),
            pltpu.VMEM((8, width), bf16),
            pltpu.VMEM((NZ, 8, width), bf16),
            pltpu.VMEM((8, width), bf16),
            pltpu.VMEM((heads, NY, 2) + key_piece[1:], bf16),
            pltpu.VMEM((heads, NY, 2) + value_piece[1:], bf16),
            pltpu.VMEM((heads, NY) + key_piece[1:], bf16),
            pltpu.VMEM((heads, NY) + value_piece[1:], bf16),
            pltpu.VMEM((NY,) + key_piece, bf16),
            pltpu.VMEM((NY,) + value_piece, bf16),
            pltpu.VMEM((2,) + half_key, bf16),
            pltpu.VMEM((2,) + half_value, bf16),
            pltpu.VMEM((2,) + key_piece, bf16),
            pltpu.VMEM((2,) + value_piece, bf16),
            pltpu.VMEM(key_piece, bf16),
            pltpu.VMEM(value_piece, bf16),
            pltpu.VMEM((heads, n_nope // 16, latent), bf16),
            pltpu.VMEM((heads, latent // 16, values), bf16),
            pltpu.SemaphoreType.DMA((n_copies,)),
            pltpu.SemaphoreType.DMA((n_copies,)),
        ],
        compiler_params=pltpu.CompilerParams(collective_id=1, has_side_effects=True),
    )(table, pos, keys, query_rows, grad_latent, nope, grad, key_up)


def on_device(
    query_nope, query_rope, query_pos, latent_cache, block_table, key_up, value_up, grad_out
):
    row_width = latent_cache.shape[3]
    nope = query_nope.reshape(-1, query_nope.shape[3])
    grad = grad_out.reshape(-1, grad_out.shape[3])
    rope = jnp.transpose(query_rope[0], (1, 2, 0))
    heads, rope_width, queries = rope.shape
    own_rows = latent_cache.reshape(-1, row_width)
    keys, query_rows, grad_latent = gather_and_project(
        own_rows, nope, grad, rope.reshape(-1, queries), key_up, value_up
    )
    grad_nope, grad_rope, cache_grad, grad_key_map, grad_value_map = attend_and_reduce(
        block_table, query_pos, keys.reshape(-1, row_width), query_rows, grad_latent, nope, grad, key_up
    )
    return (
        grad_nope.reshape(query_nope.shape),
        jnp.transpose(grad_rope.reshape(heads, rope_width, queries), (2, 0, 1))[None],
        cache_grad.reshape(latent_cache.shape),
        grad_key_map,
        grad_value_map,
    )


def solution(mesh):
    placed = (
        P("dp", "ctx", "head", None),
        P("dp", "ctx", "head", None),
        P("dp", "ctx"),
        P("dp", "ctx", None, None),
        P("dp", None),
        P("head", None, None),
        P("head", None, None),
        P("dp", "ctx", "head", None),
    )
    return jax.shard_map(
        on_device,
        mesh=mesh,
        in_specs=placed,
        out_specs=(
            P("dp", "ctx", "head", None),
            P("dp", "ctx", "head", None),
            P("dp", "ctx", None, None),
            P("head", ("ctx", "dp"), None),
            P("head", ("ctx", "dp"), None),
        ),
        check_vma=False,
    )
```

time: 96.9 us -> 72.9 us (0.75)
  matrix products: 18.1 us -> 0 us
  other arithmetic: 4.66 us -> 0 us
  local copies, waits for them, and re-layouts: 10.1 us -> 6.26 us
  Pallas kernels: 62.1 us -> 65.1 us
    dot_general x9 -> x0, matrix products: 13.8 us -> none  [the longest x1 3.7 us: on_device(): jnp.einsum('hql,qhv->hlv', attn_out, grad_out[0], preferred_element_type=...]
    sub x1 -> x0, matrix products: 4.28 us -> none  [on_device(): weights = jnp.exp(scores - jnp.max(scores, axis=2, keepdims=True))]
    convert_element_type x1 -> x0, other arithmetic: 3.03 us -> none  [on_device(): (attn_probs * (grad_probs - row_delta) * softmax_scale).astype(bf16)]
    pallas_call x2, Pallas kernels: 62.1 us -> 65.1 us  [the longest x1 48 us: attend_and_reduce(): pl.pallas_call(main_kernel, out_shape=(jax.ShapeDtypeStruct((count, n_nop...]
    convert_element_type x1 -> x0, local copies, waits for them, and re-layouts: 1.44 us -> none  [on_device(): grad_rows.astype(bf16)]
    squeeze x1 -> x0, local copies, waits for them, and re-layouts: 1.03 us -> none  [on_device(): query_nope[0]]
    unnamed x17 -> x9, local copies, waits for them, and re-layouts: 6.96 us -> 6.26 us
where the time goes in v2:
time: 72.9 us; the launch traced here: 72 us
  Pallas kernels  65.1 us (89%)
  local copies, waits for them, and re-layouts  6.26 us (9%)
    pallas_call x1, Pallas kernels, attend_and_reduce(): pl.pallas_call(main_kernel, out_shape=(jax.ShapeDtypeStruct((count, n_nop...  48 us
    pallas_call x1, Pallas kernels, gather_and_project(): pl.pallas_call(gather_kernel, out_shape=(jax.ShapeDtypeStruct((2 * NY, ro...  17 us
    unnamed x9, local copies, waits for them, and re-layouts  6.26 us

profile of v2, /device:TPU:6, one launch (start us, length us, event | category | flops | bytes accessed | tf_op | source)
XLA Modules:
  0.0 72.0 jit_solution(3713841242293869515)
XLA Ops:
  0.6 17.0 %shard_map.119 = (bf16[8,128,576]{2,1,0:T(8,128)(2,1)}, bf16[512,576]{1,0:T(8,128)(2,1)}, bf16[512,512]{1,0:T(8,128)(2,1)}) custom-call(bf16[128,576]{1,0:T(8,128)(2,1)} %bitcast.23, bf16[512,128]{1,0:T(8,128)(2,1)} %bitcast.17, bf16[512,128]{1,0:T(8,128)(2,1)} %bitcast.19, bf16[256,128]{1,0:T(8,128)(2,1)} %bitcast.25, bf16[4,128,512]{2,1,0:T(8,128)(2,1)} %key_up_ref.3, ...), custom_call_target="tpu_custom_call" | custom-call | tf_op jit(solution)/shard_map/pallas_call | solution.py:130
  17.7 48.0 %shard_map.120 = (f32[512,128]{1,0:T(8,128)}, f32[256,128]{1,0:T(8,128)}, f32[16,8,576]{2,1,0:T(8,128)}, f32[4,8,512]{2,1,0:T(8,128)}, f32[4,32,128]{2,1,0:T(8,128)}) custom-call(s32[1,16]{1,0:T(1,128)} %table_ref.1, s32[1,128]{1,0:T(1,128)} %pos_ref.1, bf16[1024,576]{1,0:T(8,128)(2,1)} %bitcast.16, bf16[512,576]{1,0:T(8,128)(2,1)} %get-tuple-element.14.query_ref, ...), custom_call_target="tpu_custom_call" | custom-call | tf_op jit(solution)/shard_map/pallas_call | solution.py:393
  65.7 0.0 copy-start.1
  65.7 0.0 copy-start
  65.7 1.7 %copy.18 = f32[1,128,4,128]{3,2,1,0:T(4,128)} copy(f32[1,128,4,128]{3,2,1,0:T(4,128)} %bitcast.22) | data formatting | bytes 524288
  67.4 1.6 %copy.19 = f32[1,128,4,64]{1,3,2,0:T(8,128)} copy(f32[1,128,4,64]{1,3,2,0:T(8,128)} %bitcast.24) | data formatting | bytes 262144
  69.0 1.7 %copy.20 = f32[1,2,64,576]{3,2,1,0:T(8,128)} copy(f32[1,2,64,576]{3,2,1,0:T(8,128)} %bitcast.21) | data formatting | bytes 589824
  70.7 0.0 copy-done.1
  70.7 0.6 copy.21
  71.4 0.0 copy-done
  71.4 0.6 copy.22
Async XLA Ops:
  65.7 5.0 %copy-start.1 = (f32[4,8,512]{2,1,0:T(8,128)S(1)}, f32[4,8,512]{2,1,0:T(8,128)}, u32[]{:S(2)}) copy-start(f32[4,8,512]{2,1,0:T(8,128)} %get-tuple-element.29) | copy-start | bytes 196612
  65.7 5.6 %copy-start = (f32[4,32,128]{2,1,0:T(8,128)S(1)}, f32[4,32,128]{2,1,0:T(8,128)}, u32[]{:S(2)}) copy-start(f32[4,32,128]{2,1,0:T(8,128)} %get-tuple-element.30) | copy-start | bytes 196612

commit v3 on v2

--- a/solution.py
+++ b/solution.py
@@ -71,12 +71,14 @@
 ):
     ctx = lax.axis_index("ctx")
     y, core = ctx // 2, ctx % 2
+    rows_each = own_ref.shape[0]
 
     def at(step, which):
         return {"ctx": lax.rem(y + step, NY) * 2 + which}
 
     def slot(step):
-        return all_ref.at[lax.rem(y + step, NY) * 2 + core]
+        place = (lax.rem(y + step, NY) * 2 + core) * rows_each
+        return all_ref.at[pl.ds(pl.multiple_of(place, rows_each), rows_each)]
 
     ahead = 1 + 2 * core
     behind = 3 - 2 * core
@@ -130,9 +132,9 @@
     return pl.pallas_call(
         gather_kernel,
         out_shape=(
-            jax.ShapeDtypeStruct((2 * NY, rows, width), bf16),
-            jax.ShapeDtypeStruct((nope.shape[0], width), bf16),
-            jax.ShapeDtypeStruct((nope.shape[0], latent), bf16),
+            pltpu.VMEM((2 * NY * rows, width), bf16),
+            pltpu.VMEM((nope.shape[0], width), bf16),
+            pltpu.VMEM((nope.shape[0], latent), bf16),
         ),
         in_specs=[vmem] * 6,
         out_specs=(vmem,) * 3,
@@ -147,9 +149,9 @@
 
 def main_kernel(
     table_ref, pos_ref, keys_ref, query_ref, latent_ref, nope_ref, grad_ref, key_up_ref,
-    nope_out, rope_out, cache_ref, key_out, value_out,
+    nope_out, rope_out, final, key_out, value_out,
     key_pos, scores, grad_probs, score_t, prob_t, query_grad, rope_parts, out_t,
-    rows_out, pair_rows, acc, ring_half, ring_in, block, z_in, piece, piece_in, final, done,
+    rows_out, pair_rows, acc, ring_half, ring_in, block, z_in, piece, piece_in, done,
     key_part, value_part,
     pair_key, pair_value, key_acc, value_acc, key_half, value_half, key_in, value_in,
     key_sum, value_sum, key_far, value_far,
@@ -375,7 +377,6 @@
     value_out[...] = total(value_sum[:, dp], value_far[...])
     for copy in gather:
         copy.wait_recv()
-    cache_ref[...] = final[...].astype(f32)
     copies.finish()
 
 
@@ -393,11 +394,11 @@
     return pl.pallas_call(
         main_kernel,
         out_shape=(
-            jax.ShapeDtypeStruct((count, n_nope), f32),
-            jax.ShapeDtypeStruct((heads * (width - latent), count // heads), f32),
-            jax.ShapeDtypeStruct((NZ, 8, width), f32),
-            jax.ShapeDtypeStruct((heads, n_nope // 16, latent), f32),
-            jax.ShapeDtypeStruct((heads, latent // 16, values), f32),
+            pltpu.VMEM((count, n_nope), f32),
+            pltpu.VMEM((heads * (width - latent), count // heads), f32),
+            pltpu.VMEM((NZ, 8, width), bf16),
+            pltpu.VMEM((heads, n_nope // 16, latent), f32),
+            pltpu.VMEM((heads, latent // 16, values), f32),
         ),
         in_specs=[pl.BlockSpec(memory_space=pltpu.SMEM)] + [vmem] * 7,
         out_specs=(vmem,) * 5,
@@ -419,7 +420,6 @@
             pltpu.VMEM((NZ, 8, width), bf16),
             pltpu.VMEM((8, width), bf16),
             pltpu.VMEM((8, width), bf16),
-            pltpu.VMEM((NZ, 8, width), bf16),
             pltpu.VMEM((8, width), bf16),
             pltpu.VMEM((heads, NY, 2) + key_piece[1:], bf16),
             pltpu.VMEM((heads, NY, 2) + value_piece[1:], bf16),
@@ -439,7 +439,26 @@
             pltpu.SemaphoreType.DMA((n_copies,)),
         ],
         compiler_params=pltpu.CompilerParams(collective_id=1, has_side_effects=True),
-    )(table, pos, keys, query_rows, grad_latent, nope, grad, key_up)
+    )(table, pos, *in_vmem(keys, query_rows, grad_latent), nope, grad, key_up)
+
+
+def in_vmem(*arrays):
+    return [pltpu.with_memory_space_constraint(array, pltpu.VMEM) for array in arrays]
+
+
+def store_kernel(*refs):
+    for source, target in zip(refs[:5], refs[5:10]):
+        target[...] = source[...].astype(f32)
+
+
+def store_results(*results):
+    vmem = pl.BlockSpec(memory_space=pltpu.VMEM)
+    return pl.pallas_call(
+        store_kernel,
+        out_shape=tuple(jax.ShapeDtypeStruct(result.shape, f32) for result in results),
+        in_specs=[vmem] * len(results),
+        out_specs=(vmem,) * len(results),
+    )(*in_vmem(*results))
 
 
 def on_device(
@@ -454,9 +473,10 @@
     keys, query_rows, grad_latent = gather_and_project(
         own_rows, nope, grad, rope.reshape(-1, queries), key_up, value_up
     )
-    grad_nope, grad_rope, cache_grad, grad_key_map, grad_value_map = attend_and_reduce(
-        block_table, query_pos, keys.reshape(-1, row_width), query_rows, grad_latent, nope, grad, key_up
+    results = attend_and_reduce(
+        block_table, query_pos, keys, query_rows, grad_latent, nope, grad, key_up
     )
+    grad_nope, grad_rope, cache_grad, grad_key_map, grad_value_map = store_results(*results)
     return (
         grad_nope.reshape(query_nope.shape),
         jnp.transpose(grad_rope.reshape(heads, rope_width, queries), (2, 0, 1))[None],

time: 72.9 us -> 64.5 us (0.88)
  local copies, waits for them, and re-layouts: 6.26 us -> 0 us
  Pallas kernels: 65.1 us -> 62.9 us
    unnamed x9 -> x0, local copies, waits for them, and re-layouts: 6.26 us -> none
    pallas_call x2 -> x3, Pallas kernels: 65.1 us -> 62.9 us  [the longest x1 46.4 us: attend_and_reduce(): pl.pallas_call(main_kernel, out_shape=(pltpu.VMEM((count, n_nope), f32),...]
where the time goes in v3:
time: 64.5 us; the launch traced here: 63.6 us
  Pallas kernels  62.9 us (98%)
  between operations  0.65 us (1%)
    pallas_call x1, Pallas kernels, attend_and_reduce(): pl.pallas_call(main_kernel, out_shape=(pltpu.VMEM((count, n_nope), f32),...  46.4 us
    pallas_call x1, Pallas kernels, gather_and_project(): pl.pallas_call(gather_kernel, out_shape=(pltpu.VMEM((2 * NY * rows, width...  15.6 us

profile of v3, /device:TPU:6, one launch (start us, length us, event | category | flops | bytes accessed | tf_op | source)
XLA Modules:
  0.0 63.6 jit_solution(12197050612459630538)
XLA Ops:
  0.6 15.6 %shard_map.119 = (bf16[1024,576]{1,0:T(8,128)(2,1)S(1)}, bf16[512,576]{1,0:T(8,128)(2,1)S(1)}, bf16[512,512]{1,0:T(8,128)(2,1)S(1)}) custom-call(bf16[128,576]{1,0:T(8,128)(2,1)} %bitcast.19, bf16[512,128]{1,0:T(8,128)(2,1)} %bitcast.15, bf16[512,128]{1,0:T(8,128)(2,1)} %bitcast.17, bf16[256,128]{1,0:T(8,128)(2,1)} %bitcast.20, ...), custom_call_target="tpu_custom_call" | custom-call | tf_op jit(solution)/shard_map/pallas_call | solution.py:132
  16.2 46.4 %shard_map.120 = (f32[512,128]{1,0:T(8,128)S(1)}, f32[256,128]{1,0:T(8,128)S(1)}, bf16[16,8,576]{2,1,0:T(8,128)(2,1)S(1)}, f32[4,8,512]{2,1,0:T(8,128)S(1)}, f32[4,32,128]{2,1,0:T(8,128)S(1)}) custom-call(s32[1,16]{1,0:T(1,128)} %table_ref.1, s32[1,128]{1,0:T(1,128)} %pos_ref.1, bf16[1024,576]{1,0:T(8,128)(2,1)S(1)} %get-tuple-element.18.keys_ref, ...), custom_call_target="tpu_custom_call" | custom-call | tf_op jit(solution)/shard_map/pallas_call | solution.py:394
  62.6 0.9 %shard_map.121 = (f32[512,128]{1,0:T(8,128)}, f32[256,128]{1,0:T(8,128)}, f32[16,8,576]{2,1,0:T(8,128)}, f32[4,8,512]{2,1,0:T(8,128)}, f32[4,32,128]{2,1,0:T(8,128)}) custom-call(f32[512,128]{1,0:T(8,128)S(1)} %get-tuple-element.21.refs_0_, f32[256,128]{1,0:T(8,128)S(1)} %get-tuple-element.22.refs_1_, bf16[16,8,576]{2,1,0:T(8,128)(2,1)S(1)} %get-tuple-element.23.refs_2_, ...), custom_call_target="tpu_custom_call" | custom-call | tf_op jit(solution)/shard_map/pallas_call | solution.py:456

commit v4 on v3

--- a/solution.py
+++ b/solution.py
@@ -10,6 +10,7 @@
 NY = 4
 NZ = 16
 HEADS = 4
+VMEM_LIMIT = 48 * 2**20
 f32 = jnp.float32
 bf16 = jnp.bfloat16
 
@@ -64,39 +65,61 @@
     return jnp.where(lax.rem(iota(values.shape, 0), HEADS) == head, values.astype(f32), 0.0).astype(bf16)
 
 
+def fetch(sources, targets, sems):
+    copies = []
+    for at, (source, target) in enumerate(zip(sources, targets)):
+        copies.append(pltpu.make_async_copy(source, target, sems.at[at]))
+        copies[-1].start()
+    return copies
+
+
 def gather_kernel(
-    own_ref, nope_ref, grad_ref, rope_ref, key_up_ref, value_up_ref,
-    all_ref, query_ref, latent_ref,
-    send_sems, recv_sems, own_sem,
+    table_ref, pos_ref, own_ref, nope_hbm, grad_hbm, rope_hbm, key_up_hbm, value_up_hbm,
+    all_ref, query_ref, latent_ref, scores, grad_probs, row_max,
+    nope_ref, grad_ref, rope_ref, key_up_ref, value_up_ref,
+    send_sems, recv_sems, own_sem, fetch_sems,
 ):
+    fetches = fetch(
+        [nope_hbm, key_up_hbm, rope_hbm, grad_hbm, value_up_hbm],
+        [nope_ref, key_up_ref, rope_ref, grad_ref, value_up_ref],
+        fetch_sems,
+    )
     ctx = lax.axis_index("ctx")
     y, core = ctx // 2, ctx % 2
     rows_each = own_ref.shape[0]
+    half = rows_each // 2
 
     def at(step, which):
         return {"ctx": lax.rem(y + step, NY) * 2 + which}
 
-    def slot(step):
-        place = (lax.rem(y + step, NY) * 2 + core) * rows_each
-        return all_ref.at[pl.ds(pl.multiple_of(place, rows_each), rows_each)]
+    def place(step, which):
+        return pl.multiple_of((lax.rem(y + step, NY) * 2 + which) * rows_each, rows_each)
+
+    def slot(step, part):
+        return all_ref.at[pl.ds(pl.multiple_of(place(step, core) + part * half, half), half)]
 
     ahead = 1 + 2 * core
     behind = 3 - 2 * core
     sibling = at(0, 1 - core)
     entry_barrier([sibling, at(1, core), at(3, core)])
     copies = Copies(send_sems, recv_sems)
-    to_ahead = copies.start(own_ref, slot(0), at(ahead, core))
-    to_behind = copies.start(own_ref, slot(0), at(behind, core))
-    to_sibling = [copies.start(own_ref, slot(0), sibling)]
-    keep = pltpu.make_async_copy(own_ref, slot(0), own_sem)
+    halves = range(2)
+    to_ahead, to_behind = [], []
+    for part in halves:
+        mine = own_ref.at[pl.ds(part * half, half)]
+        to_ahead.append(copies.start(mine, slot(0, part), at(ahead, core)))
+        to_behind.append(copies.start(mine, slot(0, part), at(behind, core)))
+    own_slot = all_ref.at[pl.ds(place(0, core), rows_each)]
+    pair_own = copies.start(own_ref, own_slot, sibling)
+    keep = pltpu.make_async_copy(own_ref, own_slot, own_sem)
     keep.start()
 
     latent = key_up_ref.shape[2]
     rope = rope_ref.shape[0] // HEADS
-
-    @pl.loop(0, nope_ref.shape[0] // 128)
-    def _(step):
-        rows = pl.ds(step * 128, 128)
+    count = nope_ref.shape[0]
+
+    def project(step):
+        rows = slice(step * 128, (step + 1) * 128)
         nope, grad = nope_ref[rows, :], grad_ref[rows, :]
         spread = jnp.concatenate([one_head(nope, head) for head in range(HEADS)], axis=1)
         up = key_up_ref[...].reshape(spread.shape[1], latent)
@@ -112,50 +135,111 @@
         fold = (lax.rem(iota((shape[1], rope), 0), rope) == iota((shape[1], rope), 1)).astype(f32).astype(bf16)
         query_ref[rows, latent:] = dot(jnp.where(mine, every, 0.0).astype(bf16), fold, 1, 0).astype(bf16)
 
-    to_ahead.wait_recv()
-    onward = copies.start(slot(behind), slot(behind), at(ahead, core))
-    to_sibling.append(copies.start(slot(behind), slot(behind), sibling))
-    to_behind.wait_recv()
-    to_sibling.append(copies.start(slot(ahead), slot(ahead), sibling))
-    onward.wait_recv()
-    to_sibling.append(copies.start(slot(2), slot(2), sibling))
-    for copy in to_sibling:
-        copy.wait_recv()
+    for copy in fetches:
+        copy.wait()
+    project(0)
+    project(1)
+    project(2)
+    onward, from_behind, from_ahead = [], [], []
+    for part in halves:
+        to_ahead[part].wait_recv()
+        onward.append(copies.start(slot(behind, part), slot(behind, part), at(ahead, core)))
+        from_behind.append(copies.start(slot(behind, part), slot(behind, part), sibling))
+        to_behind[part].wait_recv()
+        from_ahead.append(copies.start(slot(ahead, part), slot(ahead, part), sibling))
+        if part == 0:
+            project(3)
+
+    blocks = table_ref.shape[1]
+    page = all_ref.shape[0] // blocks
+    spread = (iota((count // HEADS, count), 0) == iota((count // HEADS, count), 1) // HEADS).astype(f32).astype(bf16)
+    pos = jnp.broadcast_to(pos_ref[...], (8, count // HEADS))
+    query_pos = (
+        dot((pos // 32).astype(f32).astype(bf16), spread, 1, 0) * 32.0
+        + dot(lax.rem(pos, 32).astype(f32).astype(bf16), spread, 1, 0)
+    )
+    row_max[...] = jnp.full(row_max.shape, -jnp.inf, f32)
+
+    def score(source, first, start):
+        rows = pl.ds(start, rows_each)
+        keys = source[pl.ds(first, rows_each), :]
+        raw = dot(keys, query_ref[...], 1, 1) * softmax_scale
+        index = iota((rows_each, 1), 0)
+        key_pos = lax.rem(index, page)
+        for part in range(rows_each // page):
+            here = start // page + part
+            base = sum(jnp.where(table_ref[0, b] == here, b * page, 0) for b in range(blocks))
+            key_pos = key_pos + jnp.where(index // page == part, base, 0)
+        raw = jnp.where(key_pos.astype(f32) <= query_pos[0:1, :], raw, -jnp.inf)
+        scores[rows, :] = raw
+        grad_probs[rows, :] = dot(keys[:, :latent], latent_ref[...], 1, 1)
+        row_max[...] = jnp.maximum(row_max[...], jnp.max(raw, axis=0, keepdims=True))
+
     keep.wait()
+    score(all_ref, place(0, core), place(0, core))
+    pair_own.wait_recv()
+    score(all_ref, place(0, 1 - core), place(0, 1 - core))
+    score(all_ref, place(behind, core), place(behind, core))
+    onward[0].wait_recv()
+    far = [copies.start(slot(2, 0), slot(2, 0), sibling)]
+    score(all_ref, place(ahead, core), place(ahead, core))
+    onward[1].wait_recv()
+    far.append(copies.start(slot(2, 1), slot(2, 1), sibling))
+    for copy in from_behind:
+        copy.wait_recv()
+    score(all_ref, place(ahead, 1 - core), place(ahead, 1 - core))
+    for copy in from_ahead:
+        copy.wait_recv()
+    score(all_ref, place(behind, 1 - core), place(behind, 1 - core))
+    score(all_ref, place(2, core), place(2, core))
+    for copy in far:
+        copy.wait_recv()
+    score(all_ref, place(2, 1 - core), place(2, 1 - core))
     copies.finish()
 
 
-def gather_and_project(own_rows, nope, grad, rope, key_up, value_up):
+def gather_and_score(table, pos, own_rows, nope, grad, rope, key_up, value_up):
     rows, width = own_rows.shape
     latent = key_up.shape[2]
+    count = nope.shape[0]
+    n_keys = 2 * NY * rows
     vmem = pl.BlockSpec(memory_space=pltpu.VMEM)
+    hbm = pl.BlockSpec(memory_space=pltpu.HBM)
     return pl.pallas_call(
         gather_kernel,
         out_shape=(
-            pltpu.VMEM((2 * NY * rows, width), bf16),
-            pltpu.VMEM((nope.shape[0], width), bf16),
-            pltpu.VMEM((nope.shape[0], latent), bf16),
+            pltpu.VMEM((n_keys, width), bf16),
+            pltpu.VMEM((count, width), bf16),
+            pltpu.VMEM((count, latent), bf16),
+            pltpu.VMEM((n_keys, count), f32),
+            pltpu.VMEM((n_keys, count), f32),
+            pltpu.VMEM((1, count), f32),
         ),
-        in_specs=[vmem] * 6,
-        out_specs=(vmem,) * 3,
-        scratch_shapes=[
-            pltpu.SemaphoreType.DMA((7,)),
-            pltpu.SemaphoreType.DMA((7,)),
+        in_specs=[pl.BlockSpec(memory_space=pltpu.SMEM), vmem] + [hbm] * 6,
+        out_specs=(vmem,) * 6,
+        scratch_shapes=[pltpu.VMEM(array.shape, bf16) for array in (nope, grad, rope, key_up, value_up)]
+        + [
+            pltpu.SemaphoreType.DMA((13,)),
+            pltpu.SemaphoreType.DMA((13,)),
             pltpu.SemaphoreType.DMA,
+            pltpu.SemaphoreType.DMA((5,)),
         ],
-        compiler_params=pltpu.CompilerParams(collective_id=0, has_side_effects=True),
-    )(own_rows, nope, grad, rope, key_up, value_up)
+        compiler_params=pltpu.CompilerParams(
+            collective_id=0, has_side_effects=True, vmem_limit_bytes=VMEM_LIMIT
+        ),
+    )(table, pos, own_rows, nope, grad, rope, key_up, value_up)
 
 
 def main_kernel(
-    table_ref, pos_ref, keys_ref, query_ref, latent_ref, nope_ref, grad_ref, key_up_ref,
+    keys_ref, query_ref, latent_ref, scores, grad_probs, row_max_ref, nope_hbm, grad_hbm, key_up_hbm,
     nope_out, rope_out, final, key_out, value_out,
-    key_pos, scores, grad_probs, score_t, prob_t, query_grad, rope_parts, out_t,
+    score_t, prob_t, query_grad, rope_parts, out_t,
     rows_out, pair_rows, acc, ring_half, ring_in, block, z_in, piece, piece_in, done,
     key_part, value_part,
     pair_key, pair_value, key_acc, value_acc, key_half, value_half, key_in, value_in,
     key_sum, value_sum, key_far, value_far,
-    send_sems, recv_sems,
+    nope_ref, grad_ref, key_up_ref,
+    send_sems, recv_sems, fetch_sems,
 ):
     ctx = lax.axis_index("ctx")
     head = lax.axis_index("head")
@@ -177,62 +261,38 @@
     for device in friends:
         pl.semaphore_signal(barrier, inc=1, device_id=device, device_id_type=MESH)
 
-    blocks = table_ref.shape[1]
-    page = keys_ref.shape[0] // blocks
-    lanes = key_pos.shape[1]
-    for slot in range(blocks):
-        start = sum(jnp.where(table_ref[0, at] == slot, at * page, 0) for at in range(blocks))
-        key_pos[slot * page:(slot + 1) * page, :] = (iota((page, lanes), 0) + start).astype(f32)
+    fetches = fetch([nope_hbm, grad_hbm, key_up_hbm], [nope_ref, grad_ref, key_up_ref], fetch_sems)
     count = query_ref.shape[0]
-    spread = (iota((count // HEADS, count), 0) == iota((count // HEADS, count), 1) // HEADS).astype(f32).astype(bf16)
-    pos = jnp.broadcast_to(pos_ref[...], (8, count // HEADS))
-    pos_high, pos_low = pos // 32, lax.rem(pos, 32)
-    query_pos = (
-        dot(pos_high.astype(f32).astype(bf16), spread, 1, 0) * 32.0
-        + dot(pos_low.astype(f32).astype(bf16), spread, 1, 0)
-    )
     latent = latent_ref.shape[1]
     width = keys_ref.shape[1]
     n_keys = keys_ref.shape[0]
-    chunk = 256
+    chunk = 64
     n_chunks = n_keys // chunk
-
-    for part in range(count // lanes):
-        mine = slice(part * lanes, (part + 1) * lanes)
-        at_pos = query_pos[0:1, mine]
-
-        def score_step(step, row_max):
-            rows = pl.ds(step * chunk, chunk)
-            raw = dot(keys_ref[rows, :], query_ref[mine, :], 1, 1) * softmax_scale
-            raw = jnp.where(key_pos[rows, :] <= at_pos, raw, -jnp.inf)
-            scores[rows, :] = raw
-            grad_probs[rows, :] = dot(keys_ref[rows, :latent], latent_ref[mine, :], 1, 1)
-            return jnp.maximum(row_max, jnp.max(raw, axis=0, keepdims=True))
-
-        row_max = lax.fori_loop(0, n_chunks, score_step, jnp.full((1, lanes), -jnp.inf, f32))
-
-        def weight_step(step, sums):
-            rows = pl.ds(step * chunk, chunk)
-            weights = jnp.exp(scores[rows, :] - row_max)
-            scores[rows, :] = weights
-            return (
-                sums[0] + jnp.sum(weights, axis=0, keepdims=True),
-                sums[1] + jnp.sum(weights * grad_probs[rows, :], axis=0, keepdims=True),
-            )
-
-        zero = jnp.zeros((1, lanes), f32)
-        denominator, weighted = lax.fori_loop(0, n_chunks, weight_step, (zero, zero))
-        scale = 1.0 / denominator
-        row_delta = weighted * scale
-
-        def grad_step(step, carry):
-            rows = pl.ds(step * chunk, chunk)
-            probs = scores[rows, :] * scale
-            prob_t[rows, mine] = probs.astype(bf16)
-            score_t[rows, mine] = (probs * (grad_probs[rows, :] - row_delta) * softmax_scale).astype(bf16)
-            return carry
-
-        lax.fori_loop(0, n_chunks, grad_step, 0)
+    row_max = row_max_ref[...]
+
+    def weight_step(step, sums):
+        rows = pl.ds(step * chunk, chunk)
+        weights = jnp.exp(scores[rows, :] - row_max)
+        pair = weights * grad_probs[rows, :]
+        return sums[0] + by_eight(weights), sums[1] + by_eight(pair)
+
+    def by_eight(values):
+        return jnp.sum(values.reshape(-1, 8, values.shape[1]), axis=0)
+
+    zero = jnp.zeros((8, count), f32)
+    sums = lax.fori_loop(0, n_chunks, weight_step, (zero, zero))
+    denominator, weighted = [jnp.sum(part, axis=0, keepdims=True) for part in sums]
+    scale = 1.0 / denominator
+    row_delta = weighted * scale
+
+    def grad_step(step, carry):
+        rows = pl.ds(step * chunk, chunk)
+        probs = jnp.exp(scores[rows, :] - row_max) * scale
+        prob_t[rows, :] = probs.astype(bf16)
+        score_t[rows, :] = (probs * (grad_probs[rows, :] - row_delta) * softmax_scale).astype(bf16)
+        return carry
+
+    lax.fori_loop(0, n_chunks, grad_step, 0)
 
     pl.semaphore_wait(barrier, len(friends))
     copies = Copies(send_sems, recv_sems)
@@ -286,6 +346,9 @@
         copy.wait_recv()
     block[...] = total(acc[0], ring_in[0], ring_in[1]).astype(bf16).reshape(block.shape)
     scatter = [copies.start(block.at[z_at[step]], z_in.at[step], z_device[step]) for step in far_first]
+
+    for copy in fetches:
+        copy.wait()
 
     @pl.loop(0, HEADS)
     def _(at):
@@ -341,6 +404,10 @@
         copies.start(key_acc.at[3, low], key_in.at[1, low], down),
         copies.start(value_acc.at[3, low], value_in.at[1, low], down),
     ]
+    for copy in scatter:
+        copy.wait_recv()
+    piece[...] = total(block[z], *[z_in[step] for step in range(1, NZ)]).astype(bf16)
+    across = copies.start(piece, piece_in, x_pair)
     for copy in weights_far:
         copy.wait_recv()
     key_acc[1, low] = total(key_acc[1, low], key_half[0]).astype(bf16)
@@ -354,10 +421,6 @@
         copies.start(value_acc.at[3, high], value_in.at[1, high], down),
     ]
 
-    for copy in scatter:
-        copy.wait_recv()
-    piece[...] = total(block[z], *[z_in[step] for step in range(1, NZ)]).astype(bf16)
-    across = copies.start(piece, piece_in, x_pair)
     across.wait_recv()
     done[...] = total(piece[...], piece_in[...]).astype(bf16)
     final[z] = done[...]
@@ -380,7 +443,7 @@
     copies.finish()
 
 
-def attend_and_reduce(table, pos, keys, query_rows, grad_latent, nope, grad, key_up):
+def attend_and_reduce(keys, query_rows, grad_latent, scores, grad_probs, row_max, nope, grad, key_up):
     n_keys, width = keys.shape
     count, n_nope = nope.shape
     heads, _, latent = key_up.shape
@@ -391,6 +454,7 @@
     half_value = (heads // 2,) + value_piece[1:]
     n_copies = 4 + 2 + 6 + 8 + 4 + 15 + 1 + 2 + 15
     vmem = pl.BlockSpec(memory_space=pltpu.VMEM)
+    hbm = pl.BlockSpec(memory_space=pltpu.HBM)
     return pl.pallas_call(
         main_kernel,
         out_shape=(
@@ -400,12 +464,9 @@
             pltpu.VMEM((heads, n_nope // 16, latent), f32),
             pltpu.VMEM((heads, latent // 16, values), f32),
         ),
-        in_specs=[pl.BlockSpec(memory_space=pltpu.SMEM)] + [vmem] * 7,
+        in_specs=[vmem] * 6 + [hbm] * 3,
         out_specs=(vmem,) * 5,
         scratch_shapes=[
-            pltpu.VMEM((n_keys, 256), f32),
-            pltpu.VMEM((n_keys, 256), f32),
-            pltpu.VMEM((n_keys, 256), f32),
             pltpu.VMEM((n_keys, count), bf16),
             pltpu.VMEM((n_keys, count), bf16),
             pltpu.VMEM((count, latent), bf16),
@@ -435,11 +496,17 @@
             pltpu.VMEM(value_piece, bf16),
             pltpu.VMEM((heads, n_nope // 16, latent), bf16),
             pltpu.VMEM((heads, latent // 16, values), bf16),
+            pltpu.VMEM(nope.shape, bf16),
+            pltpu.VMEM(grad.shape, bf16),
+            pltpu.VMEM(key_up.shape, bf16),
             pltpu.SemaphoreType.DMA((n_copies,)),
             pltpu.SemaphoreType.DMA((n_copies,)),
+            pltpu.SemaphoreType.DMA((3,)),
         ],
-        compiler_params=pltpu.CompilerParams(collective_id=1, has_side_effects=True),
-    )(table, pos, *in_vmem(keys, query_rows, grad_latent), nope, grad, key_up)
+        compiler_params=pltpu.CompilerParams(
+            collective_id=1, has_side_effects=True, vmem_limit_bytes=VMEM_LIMIT
+        ),
+    )(*in_vmem(keys, query_rows, grad_latent, scores, grad_probs, row_max), nope, grad, key_up)
 
 
 def in_vmem(*arrays):
@@ -458,6 +525,7 @@
         out_shape=tuple(jax.ShapeDtypeStruct(result.shape, f32) for result in results),
         in_specs=[vmem] * len(results),
         out_specs=(vmem,) * len(results),
+        compiler_params=pltpu.CompilerParams(vmem_limit_bytes=VMEM_LIMIT),
     )(*in_vmem(*results))
 
 
@@ -470,12 +538,10 @@
     rope = jnp.transpose(query_rope[0], (1, 2, 0))
     heads, rope_width, queries = rope.shape
     own_rows = latent_cache.reshape(-1, row_width)
-    keys, query_rows, grad_latent = gather_and_project(
-        own_rows, nope, grad, rope.reshape(-1, queries), key_up, value_up
+    shared = gather_and_score(
+        block_table, query_pos, own_rows, nope, grad, rope.reshape(-1, queries), key_up, value_up
     )
-    results = attend_and_reduce(
-        block_table, query_pos, keys, query_rows, grad_latent, nope, grad, key_up
-    )
+    results = attend_and_reduce(*shared, nope, grad, key_up)
     grad_nope, grad_rope, cache_grad, grad_key_map, grad_value_map = store_results(*results)
     return (
         grad_nope.reshape(query_nope.shape),

time: 64.5 us -> 62 us (0.961); the launches traced: 63.6 us -> 61.9 us
  Pallas kernels: 62.9 us -> 61.2 us
    pallas_call x1, Pallas kernels: 46.4 us -> 43.9 us  [attend_and_reduce(): pl.pallas_call(main_kernel, out_shape=(pltpu.VMEM((count, n_nope), f32),...]
    pallas_call x1, Pallas kernels: 15.6 us -> 16.4 us  [gather_and_score(): pl.pallas_call(gather_kernel, out_shape=(pltpu.VMEM((n_keys, width), bf16...]
where the time goes in v4:
time: 62 us; the launch traced here: 61.9 us
  Pallas kernels  61.2 us (99%)
  between operations  0.65 us (1%)
    pallas_call x1, Pallas kernels, attend_and_reduce(): pl.pallas_call(main_kernel, out_shape=(pltpu.VMEM((count, n_nope), f32),...  43.9 us
    pallas_call x1, Pallas kernels, gather_and_score(): pl.pallas_call(gather_kernel, out_shape=(pltpu.VMEM((n_keys, width), bf16...  16.4 us

profile of v4, /device:TPU:6, one launch (start us, length us, event | category | flops | bytes accessed | tf_op | source)
XLA Modules:
  0.0 61.9 jit_solution(14294394542755540736)
XLA Ops:
  0.6 16.4 %shard_map.119 = (bf16[1024,576]{1,0:T(8,128)(2,1)S(1)}, bf16[512,576]{1,0:T(8,128)(2,1)S(1)}, bf16[512,512]{1,0:T(8,128)(2,1)S(1)}, f32[1024,512]{1,0:T(8,128)S...) custom-call(s32[1,16]{1,0:T(1,128)} %table_ref.1, s32[1,128]{1,0:T(1,128)} %pos_ref.1, bf16[128,576]{1,0:T(8,128)(2,1)} %bitcast.19, ...), custom_call_target="tpu_custom_call" | custom-call | tf_op jit(solution)/shard_map/pallas_call | solution.py:208
  17.0 43.9 %shard_map.120 = (f32[512,128]{1,0:T(8,128)S(1)}, f32[256,128]{1,0:T(8,128)S(1)}, bf16[16,8,576]{2,1,0:T(8,128)(2,1)S(1)}, f32[4,8,512]{2,1,0:T(8,128)S(1)}, f32[4,32,128]{2,1,0:T(8,128)S(1)}) custom-call(bf16[1024,576]{1,0:T(8,128)(2,1)S(1)} %get-tuple-element.21.keys_ref, bf16[512,576]{1,0:T(8,128)(2,1)S(1)} %get-tuple-element.22.query_ref, ...), custom_call_target="tpu_custom_call" | custom-call | tf_op jit(solution)/shard_map/pallas_call | solution.py:458
  60.9 0.9 %shard_map.121 = (f32[512,128]{1,0:T(8,128)}, f32[256,128]{1,0:T(8,128)}, f32[16,8,576]{2,1,0:T(8,128)}, f32[4,8,512]{2,1,0:T(8,128)}, f32[4,32,128]{2,1,0:T(8,128)}) custom-call(f32[512,128]{1,0:T(8,128)S(1)} %get-tuple-element.27.refs_0_, f32[256,128]{1,0:T(8,128)S(1)} %get-tuple-element.28.refs_1_, bf16[16,8,576]{2,1,0:T(8,128)(2,1)S(1)} %get-tuple-element.29.refs_2_, ...), custom_call_target="tpu_custom_call" | custom-call | tf_op jit(solution)/shard_map/pallas_call | solution.py:523

commit v5 on v4

--- a/solution.py
+++ b/solution.py
@@ -19,13 +19,13 @@
     def __init__(self, send_sems, recv_sems):
         self.send_sems, self.recv_sems, self.made = send_sems, recv_sems, []
 
-    def start(self, src, dst, device):
+    def start(self, src, dst, device, recv_sem=None):
         at = len(self.made)
         copy = pltpu.make_async_remote_copy(
             src_ref=src,
             dst_ref=dst,
             send_sem=self.send_sems.at[at],
-            recv_sem=self.recv_sems.at[at],
+            recv_sem=self.recv_sems.at[at] if recv_sem is None else recv_sem,
             device_id=device,
             device_id_type=MESH,
         )
@@ -104,11 +104,8 @@
     entry_barrier([sibling, at(1, core), at(3, core)])
     copies = Copies(send_sems, recv_sems)
     halves = range(2)
-    to_ahead, to_behind = [], []
-    for part in halves:
-        mine = own_ref.at[pl.ds(part * half, half)]
-        to_ahead.append(copies.start(mine, slot(0, part), at(ahead, core)))
-        to_behind.append(copies.start(mine, slot(0, part), at(behind, core)))
+    own_half = [own_ref.at[pl.ds(part * half, half)] for part in halves]
+    to_ahead = [copies.start(own_half[part], slot(0, part), at(ahead, core)) for part in halves]
     own_slot = all_ref.at[pl.ds(place(0, core), rows_each)]
     pair_own = copies.start(own_ref, own_slot, sibling)
     keep = pltpu.make_async_copy(own_ref, own_slot, own_sem)
@@ -139,14 +136,13 @@
         copy.wait()
     project(0)
     project(1)
+    to_behind = [copies.start(own_half[part], slot(0, part), at(behind, core)) for part in halves]
     project(2)
-    onward, from_behind, from_ahead = [], [], []
+    onward, from_behind = [], []
     for part in halves:
         to_ahead[part].wait_recv()
         onward.append(copies.start(slot(behind, part), slot(behind, part), at(ahead, core)))
         from_behind.append(copies.start(slot(behind, part), slot(behind, part), sibling))
-        to_behind[part].wait_recv()
-        from_ahead.append(copies.start(slot(ahead, part), slot(ahead, part), sibling))
         if part == 0:
             project(3)
 
@@ -179,12 +175,16 @@
     score(all_ref, place(0, core), place(0, core))
     pair_own.wait_recv()
     score(all_ref, place(0, 1 - core), place(0, 1 - core))
+    from_ahead = []
+    for part in halves:
+        to_behind[part].wait_recv()
+        from_ahead.append(copies.start(slot(ahead, part), slot(ahead, part), sibling))
     score(all_ref, place(behind, core), place(behind, core))
-    onward[0].wait_recv()
-    far = [copies.start(slot(2, 0), slot(2, 0), sibling)]
+    far = []
+    for part in halves:
+        onward[part].wait_recv()
+        far.append(copies.start(slot(2, part), slot(2, part), sibling))
     score(all_ref, place(ahead, core), place(ahead, core))
-    onward[1].wait_recv()
-    far.append(copies.start(slot(2, 1), slot(2, 1), sibling))
     for copy in from_behind:
         copy.wait_recv()
     score(all_ref, place(ahead, 1 - core), place(ahead, 1 - core))
@@ -234,12 +234,12 @@
     keys_ref, query_ref, latent_ref, scores, grad_probs, row_max_ref, nope_hbm, grad_hbm, key_up_hbm,
     nope_out, rope_out, final, key_out, value_out,
     score_t, prob_t, query_grad, rope_parts, out_t,
-    rows_out, pair_rows, acc, ring_half, ring_in, block, z_in, piece, piece_in, done,
+    rows_out, pair_rows, acc, ring_half, ring_in, own_in, block, z_in, done,
     key_part, value_part,
     pair_key, pair_value, key_acc, value_acc, key_half, value_half, key_in, value_in,
     key_sum, value_sum, key_far, value_far,
     nope_ref, grad_ref, key_up_ref,
-    send_sems, recv_sems, fetch_sems,
+    send_sems, recv_sems, fetch_sems, ring_sems, cross_sems,
 ):
     ctx = lax.axis_index("ctx")
     head = lax.axis_index("head")
@@ -254,9 +254,16 @@
     z_at = [lax.rem(z + step, NZ) for step in range(NZ)]
     z_device = [{"head": x_lo * NZ + place} for place in z_at]
     x_pair = {"head": (1 - x_lo) * NZ + z}
+    x_device = [{"head": (1 - x_lo) * NZ + place} for place in z_at]
+    up_to = [{"ctx": chips[1] * 2 + core, "head": x * NZ + z} for x in range(2)]
+    down_to = [{"ctx": chips[3] * 2 + core, "head": x * NZ + z} for x in range(2)]
+    up_across = {"ctx": chips[1] * 2 + core, "head": (1 - x_lo) * NZ + z}
+    down_across = {"ctx": chips[3] * 2 + core, "head": (1 - x_lo) * NZ + z}
     dp_pair = {"dp": 1 - dp}
     far_first = sorted(range(1, NZ), key=lambda step: -min(step, NZ - step))
-    friends = [z_device[step] for step in far_first] + [x_pair, dp_pair, up, down, sibling]
+    direct = far_first[:5]
+    friends = [z_device[step] for step in far_first] + [x_device[step] for step in direct]
+    friends += [x_pair, dp_pair, up_across, down_across, up, down, sibling]
     barrier = pltpu.get_barrier_semaphore()
     for device in friends:
         pl.semaphore_signal(barrier, inc=1, device_id=device, device_id_type=MESH)
@@ -322,16 +329,17 @@
     up_far = copies.start(acc.at[2, 0], ring_half.at[0], up)
     down_far = copies.start(acc.at[2, 1], ring_half.at[1], down)
     join(1)
-    up_own = copies.start(acc.at[1, 1], ring_in.at[0, 1], up)
+    copies.start(acc.at[1, 1], ring_in.at[0, x_lo], up_to[1], ring_sems.at[x_lo])
     join(3)
-    down_own = copies.start(acc.at[3, 0], ring_in.at[1, 0], down)
+    copies.start(acc.at[3, 0], ring_in.at[1, x_lo], down_to[0], ring_sems.at[2 + x_lo])
     join(0)
+    across = copies.start(acc.at[0, 1 - x_lo], own_in, x_pair)
     up_far.wait_recv()
     acc[1, 0] = total(acc[1, 0], ring_half[0]).astype(bf16)
-    up_both = copies.start(acc.at[1, 0], ring_in.at[0, 0], up)
+    copies.start(acc.at[1, 0], ring_in.at[0, x_lo], up_to[0], ring_sems.at[x_lo])
     down_far.wait_recv()
     acc[3, 1] = total(acc[3, 1], ring_half[1]).astype(bf16)
-    down_both = copies.start(acc.at[3, 1], ring_in.at[1, 1], down)
+    copies.start(acc.at[3, 1], ring_in.at[1, x_lo], down_to[1], ring_sems.at[2 + x_lo])
 
     @pl.loop(0, count // 128)
     def _(step):
@@ -342,9 +350,21 @@
         rope_parts[lane, :width - latent] = rope_high
         rope_parts[lane, width - latent:] = (grad[:, latent:] - rope_high.astype(f32)).astype(bf16)
 
-    for copy in (up_own, down_own, up_both, down_both):
-        copy.wait_recv()
-    block[...] = total(acc[0], ring_in[0], ring_in[1]).astype(bf16).reshape(block.shape)
+    across.wait_recv()
+    for way in range(2):
+        for x in range(2):
+            pltpu.make_async_remote_copy(
+                src_ref=ring_in.at[way, x],
+                dst_ref=ring_in.at[way, x],
+                send_sem=send_sems.at[0],
+                recv_sem=ring_sems.at[way * 2 + x],
+                device_id=x_pair,
+                device_id_type=MESH,
+            ).wait_recv()
+    mine = total(acc[0, x_lo], own_in[...], ring_in[0, 0], ring_in[0, 1], ring_in[1, 0], ring_in[1, 1])
+    piece_rows = block.shape[1]
+    for at in range(NZ):
+        block[at] = mine[at * piece_rows:(at + 1) * piece_rows].astype(bf16)
     scatter = [copies.start(block.at[z_at[step]], z_in.at[step], z_device[step]) for step in far_first]
 
     for copy in fetches:
@@ -406,8 +426,15 @@
     ]
     for copy in scatter:
         copy.wait_recv()
-    piece[...] = total(block[z], *[z_in[step] for step in range(1, NZ)]).astype(bf16)
-    across = copies.start(piece, piece_in, x_pair)
+    done[...] = total(block[z], *[z_in[step] for step in range(1, NZ)]).astype(bf16)
+    final[x_lo, z] = done[...]
+    gather = {}
+    crossed = []
+    for step in far_first:
+        gather[step] = copies.start(done, final.at[x_lo, z], z_device[step])
+        if step in direct:
+            crossed.append(copies.start(done, final.at[x_lo, z], x_device[step], cross_sems.at[step]))
+    crossed.append(copies.start(done, final.at[x_lo, z], x_pair, cross_sems.at[0]))
     for copy in weights_far:
         copy.wait_recv()
     key_acc[1, low] = total(key_acc[1, low], key_half[0]).astype(bf16)
@@ -421,10 +448,15 @@
         copies.start(value_acc.at[3, high], value_in.at[1, high], down),
     ]
 
-    across.wait_recv()
-    done[...] = total(piece[...], piece_in[...]).astype(bf16)
-    final[z] = done[...]
-    gather = [copies.start(done, final.at[z], z_device[step]) for step in far_first]
+    def pass_on(steps):
+        for step in steps:
+            gather[step].wait_recv()
+            if step not in direct:
+                come = final.at[x_lo, z_at[NZ - step]]
+                crossed.append(copies.start(come, come, x_pair, cross_sems.at[step]))
+
+    near_first = far_first[::-1]
+    pass_on(near_first[:6])
 
     for copy in weights_in:
         copy.wait_recv()
@@ -434,11 +466,12 @@
         copies.start(key_sum.at[:, 1 - dp], key_far, dp_pair),
         copies.start(value_sum.at[:, 1 - dp], value_far, dp_pair),
     ]
+    pass_on(near_first[6:])
     for copy in weights_pair:
         copy.wait_recv()
     key_out[...] = total(key_sum[:, dp], key_far[...])
     value_out[...] = total(value_sum[:, dp], value_far[...])
-    for copy in gather:
+    for copy in crossed:
         copy.wait_recv()
     copies.finish()
 
@@ -452,7 +485,7 @@
     value_piece = (heads, 2, latent // 16, values)
     half_key = (heads // 2,) + key_piece[1:]
     half_value = (heads // 2,) + value_piece[1:]
-    n_copies = 4 + 2 + 6 + 8 + 4 + 15 + 1 + 2 + 15
+    n_copies = 4 + 2 + 4 + 1 + 15 + 31 + 16
     vmem = pl.BlockSpec(memory_space=pltpu.VMEM)
     hbm = pl.BlockSpec(memory_space=pltpu.HBM)
     return pl.pallas_call(
@@ -460,7 +493,7 @@
         out_shape=(
             pltpu.VMEM((count, n_nope), f32),
             pltpu.VMEM((heads * (width - latent), count // heads), f32),
-            pltpu.VMEM((NZ, 8, width), bf16),
+            pltpu.VMEM((2, NZ, 4, width), bf16),
             pltpu.VMEM((heads, n_nope // 16, latent), f32),
             pltpu.VMEM((heads, latent // 16, values), f32),
         ),
@@ -477,11 +510,10 @@
             pltpu.VMEM((NY, 2, 64, width), bf16),
             pltpu.VMEM((2, 64, width), bf16),
             pltpu.VMEM((2, 2, 64, width), bf16),
-            pltpu.VMEM((NZ, 8, width), bf16),
-            pltpu.VMEM((NZ, 8, width), bf16),
-            pltpu.VMEM((8, width), bf16),
-            pltpu.VMEM((8, width), bf16),
-            pltpu.VMEM((8, width), bf16),
+            pltpu.VMEM((64, width), bf16),
+            pltpu.VMEM((NZ, 4, width), bf16),
+            pltpu.VMEM((NZ, 4, width), bf16),
+            pltpu.VMEM((4, width), bf16),
             pltpu.VMEM((heads, NY, 2) + key_piece[1:], bf16),
             pltpu.VMEM((heads, NY, 2) + value_piece[1:], bf16),
             pltpu.VMEM((heads, NY) + key_piece[1:], bf16),
@@ -502,6 +534,8 @@
             pltpu.SemaphoreType.DMA((n_copies,)),
             pltpu.SemaphoreType.DMA((n_copies,)),
             pltpu.SemaphoreType.DMA((3,)),
+            pltpu.SemaphoreType.DMA((4,)),
+            pltpu.SemaphoreType.DMA((NZ,)),
         ],
         compiler_params=pltpu.CompilerParams(
             collective_id=1, has_side_effects=True, vmem_limit_bytes=VMEM_LIMIT
@@ -515,14 +549,26 @@
 
 def store_kernel(*refs):
     for source, target in zip(refs[:5], refs[5:10]):
-        target[...] = source[...].astype(f32)
+        if source.dtype == bf16:
+            for half in range(source.shape[0]):
+                for at in range(source.shape[1]):
+                    rows = source.shape[2]
+                    first = (half * source.shape[1] + at) * rows
+                    target[first:first + rows, :] = source[half, at].astype(f32)
+        else:
+            target[...] = source[...]
 
 
 def store_results(*results):
     vmem = pl.BlockSpec(memory_space=pltpu.VMEM)
     return pl.pallas_call(
         store_kernel,
-        out_shape=tuple(jax.ShapeDtypeStruct(result.shape, f32) for result in results),
+        out_shape=tuple(
+            jax.ShapeDtypeStruct(result.shape, f32)
+            if result.dtype != bf16
+            else jax.ShapeDtypeStruct((result.size // result.shape[3], result.shape[3]), f32)
+            for result in results
+        ),
         in_specs=[vmem] * len(results),
         out_specs=(vmem,) * len(results),
         compiler_params=pltpu.CompilerParams(vmem_limit_bytes=VMEM_LIMIT),

time: 62 us -> 65.7 us (1.060); the launches traced: 61.9 us -> 64.5 us
  Pallas kernels: 61.2 us -> 63.8 us
    pallas_call x1, Pallas kernels: 43.9 us -> 46.1 us  [attend_and_reduce(): pl.pallas_call(main_kernel, out_shape=(pltpu.VMEM((count, n_nope), f32),...]
where the time goes in v5:
time: 65.7 us; the launch traced here: 64.5 us
  Pallas kernels  63.8 us (97%)
    pallas_call x1, Pallas kernels, attend_and_reduce(): pl.pallas_call(main_kernel, out_shape=(pltpu.VMEM((count, n_nope), f32),...  46.1 us
    pallas_call x1, Pallas kernels, gather_and_score(): pl.pallas_call(gather_kernel, out_shape=(pltpu.VMEM((n_keys, width), bf16...  16.8 us

profile of v5, /device:TPU:6, one launch (start us, length us, event | category | flops | bytes accessed | tf_op | source)
XLA Modules:
  0.0 64.5 jit_solution(10142025666810650290)
XLA Ops:
  0.6 16.8 %shard_map.119 = (bf16[1024,576]{1,0:T(8,128)(2,1)S(1)}, bf16[512,576]{1,0:T(8,128)(2,1)S(1)}, bf16[512,512]{1,0:T(8,128)(2,1)S(1)}, f32[1024,512]{1,0:T(8,128)S...) custom-call(s32[1,16]{1,0:T(1,128)} %table_ref.1, s32[1,128]{1,0:T(1,128)} %pos_ref.1, bf16[128,576]{1,0:T(8,128)(2,1)} %bitcast.19, ...), custom_call_target="tpu_custom_call" | custom-call | tf_op jit(solution)/shard_map/pallas_call | solution.py:208
  17.4 46.1 %shard_map.120 = (f32[512,128]{1,0:T(8,128)S(1)}, f32[256,128]{1,0:T(8,128)S(1)}, bf16[2,16,4,576]{3,2,1,0:T(4,128)(2,1)S(1)}, f32[4,8,512]{2,1,0:T(8,128)S(1)}, f32[4,32,128]{2,1,0:T(8,128)S(1)}) custom-call(bf16[1024,576]{1,0:T(8,128)(2,1)S(1)} %get-tuple-element.21.keys_ref, bf16[512,576]{1,0:T(8,128)(2,1)S(1)} %get-tuple-element.22.query_ref, ...), custom_call_target="tpu_custom_call" | custom-call | tf_op jit(solution)/shard_map/pallas_call | solution.py:491
  63.5 0.9 %shard_map.121 = (f32[512,128]{1,0:T(8,128)}, f32[256,128]{1,0:T(8,128)}, f32[128,576]{1,0:T(8,128)}, f32[4,8,512]{2,1,0:T(8,128)}, f32[4,32,128]{2,1,0:T(8,128)}) custom-call(f32[512,128]{1,0:T(8,128)S(1)} %get-tuple-element.27.refs_0_, f32[256,128]{1,0:T(8,128)S(1)} %get-tuple-element.28.refs_1_, bf16[2,16,4,576]{3,2,1,0:T(4,128)(2,1)S(1)} %get-tuple-element.29.refs_2_, ...), custom_call_target="tpu_custom_call" | custom-call | tf_op jit(solution)/shard_map/pallas_call | solution.py:564

commit v6 on v5

--- a/solution.py
+++ b/solution.py
@@ -74,14 +74,14 @@
 
 
 def gather_kernel(
-    table_ref, pos_ref, own_ref, nope_hbm, grad_hbm, rope_hbm, key_up_hbm, value_up_hbm,
+    table_hbm, pos_hbm, own_ref, nope_hbm, grad_hbm, rope_hbm, key_up_hbm, value_up_hbm,
     all_ref, query_ref, latent_ref, scores, grad_probs, row_max,
-    nope_ref, grad_ref, rope_ref, key_up_ref, value_up_ref,
+    table_ref, pos_ref, nope_ref, grad_ref, rope_ref, key_up_ref, value_up_ref,
     send_sems, recv_sems, own_sem, fetch_sems,
 ):
     fetches = fetch(
-        [nope_hbm, key_up_hbm, rope_hbm, grad_hbm, value_up_hbm],
-        [nope_ref, key_up_ref, rope_ref, grad_ref, value_up_ref],
+        [nope_hbm, key_up_hbm, rope_hbm, grad_hbm, value_up_hbm, table_hbm, pos_hbm],
+        [nope_ref, key_up_ref, rope_ref, grad_ref, value_up_ref, table_ref, pos_ref],
         fetch_sems,
     )
     ctx = lax.axis_index("ctx")
@@ -215,14 +215,15 @@
             pltpu.VMEM((n_keys, count), f32),
             pltpu.VMEM((1, count), f32),
         ),
-        in_specs=[pl.BlockSpec(memory_space=pltpu.SMEM), vmem] + [hbm] * 6,
+        in_specs=[hbm] * 8,
         out_specs=(vmem,) * 6,
-        scratch_shapes=[pltpu.VMEM(array.shape, bf16) for array in (nope, grad, rope, key_up, value_up)]
+        scratch_shapes=[pltpu.SMEM(table.shape, jnp.int32), pltpu.VMEM(pos.shape, jnp.int32)]
+        + [pltpu.VMEM(array.shape, bf16) for array in (nope, grad, rope, key_up, value_up)]
         + [
             pltpu.SemaphoreType.DMA((13,)),
             pltpu.SemaphoreType.DMA((13,)),
             pltpu.SemaphoreType.DMA,
-            pltpu.SemaphoreType.DMA((5,)),
+            pltpu.SemaphoreType.DMA((7,)),
         ],
         compiler_params=pltpu.CompilerParams(
             collective_id=0, has_side_effects=True, vmem_limit_bytes=VMEM_LIMIT
@@ -234,12 +235,12 @@
     keys_ref, query_ref, latent_ref, scores, grad_probs, row_max_ref, nope_hbm, grad_hbm, key_up_hbm,
     nope_out, rope_out, final, key_out, value_out,
     score_t, prob_t, query_grad, rope_parts, out_t,
-    rows_out, pair_rows, acc, ring_half, ring_in, own_in, block, z_in, done,
+    rows_out, pair_rows, acc, ring_half, ring_in, block, z_in, done,
     key_part, value_part,
     pair_key, pair_value, key_acc, value_acc, key_half, value_half, key_in, value_in,
     key_sum, value_sum, key_far, value_far,
     nope_ref, grad_ref, key_up_ref,
-    send_sems, recv_sems, fetch_sems, ring_sems, cross_sems,
+    send_sems, recv_sems, fetch_sems, cross_sems,
 ):
     ctx = lax.axis_index("ctx")
     head = lax.axis_index("head")
@@ -255,15 +256,11 @@
     z_device = [{"head": x_lo * NZ + place} for place in z_at]
     x_pair = {"head": (1 - x_lo) * NZ + z}
     x_device = [{"head": (1 - x_lo) * NZ + place} for place in z_at]
-    up_to = [{"ctx": chips[1] * 2 + core, "head": x * NZ + z} for x in range(2)]
-    down_to = [{"ctx": chips[3] * 2 + core, "head": x * NZ + z} for x in range(2)]
-    up_across = {"ctx": chips[1] * 2 + core, "head": (1 - x_lo) * NZ + z}
-    down_across = {"ctx": chips[3] * 2 + core, "head": (1 - x_lo) * NZ + z}
     dp_pair = {"dp": 1 - dp}
     far_first = sorted(range(1, NZ), key=lambda step: -min(step, NZ - step))
     direct = far_first[:5]
-    friends = [z_device[step] for step in far_first] + [x_device[step] for step in direct]
-    friends += [x_pair, dp_pair, up_across, down_across, up, down, sibling]
+    friends = [z_device[step] for step in far_first] + [x_device[step] for step in far_first]
+    friends += [x_pair, dp_pair, up, down, sibling]
     barrier = pltpu.get_barrier_semaphore()
     for device in friends:
         pl.semaphore_signal(barrier, inc=1, device_id=device, device_id_type=MESH)
@@ -329,17 +326,10 @@
     up_far = copies.start(acc.at[2, 0], ring_half.at[0], up)
     down_far = copies.start(acc.at[2, 1], ring_half.at[1], down)
     join(1)
-    copies.start(acc.at[1, 1], ring_in.at[0, x_lo], up_to[1], ring_sems.at[x_lo])
+    up_own = copies.start(acc.at[1, 1], ring_in.at[0, 1], up)
     join(3)
-    copies.start(acc.at[3, 0], ring_in.at[1, x_lo], down_to[0], ring_sems.at[2 + x_lo])
+    down_own = copies.start(acc.at[3, 0], ring_in.at[1, 0], down)
     join(0)
-    across = copies.start(acc.at[0, 1 - x_lo], own_in, x_pair)
-    up_far.wait_recv()
-    acc[1, 0] = total(acc[1, 0], ring_half[0]).astype(bf16)
-    copies.start(acc.at[1, 0], ring_in.at[0, x_lo], up_to[0], ring_sems.at[x_lo])
-    down_far.wait_recv()
-    acc[3, 1] = total(acc[3, 1], ring_half[1]).astype(bf16)
-    copies.start(acc.at[3, 1], ring_in.at[1, x_lo], down_to[1], ring_sems.at[2 + x_lo])
 
     @pl.loop(0, count // 128)
     def _(step):
@@ -350,23 +340,6 @@
         rope_parts[lane, :width - latent] = rope_high
         rope_parts[lane, width - latent:] = (grad[:, latent:] - rope_high.astype(f32)).astype(bf16)
 
-    across.wait_recv()
-    for way in range(2):
-        for x in range(2):
-            pltpu.make_async_remote_copy(
-                src_ref=ring_in.at[way, x],
-                dst_ref=ring_in.at[way, x],
-                send_sem=send_sems.at[0],
-                recv_sem=ring_sems.at[way * 2 + x],
-                device_id=x_pair,
-                device_id_type=MESH,
-            ).wait_recv()
-    mine = total(acc[0, x_lo], own_in[...], ring_in[0, 0], ring_in[0, 1], ring_in[1, 0], ring_in[1, 1])
-    piece_rows = block.shape[1]
-    for at in range(NZ):
-        block[at] = mine[at * piece_rows:(at + 1) * piece_rows].astype(bf16)
-    scatter = [copies.start(block.at[z_at[step]], z_in.at[step], z_device[step]) for step in far_first]
-
     for copy in fetches:
         copy.wait()
 
@@ -377,6 +350,13 @@
 
     pair_weights = [copies.start(key_part.at[:, :, 1 - core], pair_key, sibling)]
 
+    up_far.wait_recv()
+    acc[1, 0] = total(acc[1, 0], ring_half[0]).astype(bf16)
+    up_both = copies.start(acc.at[1, 0], ring_in.at[0, 0], up)
+    down_far.wait_recv()
+    acc[3, 1] = total(acc[3, 1], ring_half[1]).astype(bf16)
+    down_both = copies.start(acc.at[3, 1], ring_in.at[1, 1], down)
+
     @pl.loop(0, latent // 128)
     def _(step):
         lane = pl.ds(pl.multiple_of(step * 128, 128), 128)
@@ -389,22 +369,18 @@
 
     pair_weights.append(copies.start(value_part.at[:, :, 1 - core], pair_value, sibling))
 
-    @pl.loop(0, count // 128)
-    def _(step):
-        rows = pl.ds(step * 128, 128)
-        every = dot(query_grad[rows, :], key_up_ref[...].reshape(-1, latent), 1, 1)
-        n = nope_out.shape[1]
-        which = lax.rem(iota((128, n), 0), HEADS)
-        nope_out[rows, :] = total(
-            *[jnp.where(which == at, every[:, at * n:(at + 1) * n], 0.0) for at in range(HEADS)]
-        )
-
-    rope = width - latent
-    queries = count // HEADS
-    for at in range(HEADS):
-        order = (iota((count, queries), 0) == iota((count, queries), 1) * HEADS + at).astype(f32).astype(bf16)
-        turned = dot(rope_parts[...], order, 0, 0)
-        rope_out[at * rope:(at + 1) * rope, :] = turned[:rope] + turned[rope:]
+    for copy in (up_own, down_own, up_both, down_both):
+        copy.wait_recv()
+    piece_rows = block.shape[2]
+    for half in range(2):
+        mine = total(acc[0, half], ring_in[0, half], ring_in[1, half])
+        for at in range(NZ):
+            block[half, at] = mine[at * piece_rows:(at + 1) * piece_rows].astype(bf16)
+    scatter = []
+    for step in far_first + [0]:
+        if step:
+            scatter.append(copies.start(block.at[x_lo, z_at[step]], z_in.at[0, step], z_device[step]))
+        scatter.append(copies.start(block.at[1 - x_lo, z_at[step]], z_in.at[1, step], x_device[step]))
 
     for copy in pair_weights:
         copy.wait_recv()
@@ -424,17 +400,23 @@
         copies.start(key_acc.at[3, low], key_in.at[1, low], down),
         copies.start(value_acc.at[3, low], value_in.at[1, low], down),
     ]
-    for copy in scatter:
-        copy.wait_recv()
-    done[...] = total(block[z], *[z_in[step] for step in range(1, NZ)]).astype(bf16)
-    final[x_lo, z] = done[...]
-    gather = {}
-    crossed = []
-    for step in far_first:
-        gather[step] = copies.start(done, final.at[x_lo, z], z_device[step])
-        if step in direct:
-            crossed.append(copies.start(done, final.at[x_lo, z], x_device[step], cross_sems.at[step]))
-    crossed.append(copies.start(done, final.at[x_lo, z], x_pair, cross_sems.at[0]))
+    @pl.loop(0, count // 128)
+    def _(step):
+        rows = pl.ds(step * 128, 128)
+        every = dot(query_grad[rows, :], key_up_ref[...].reshape(-1, latent), 1, 1)
+        n = nope_out.shape[1]
+        which = lax.rem(iota((128, n), 0), HEADS)
+        nope_out[rows, :] = total(
+            *[jnp.where(which == at, every[:, at * n:(at + 1) * n], 0.0) for at in range(HEADS)]
+        )
+
+    rope = width - latent
+    queries = count // HEADS
+    for at in range(HEADS):
+        order = (iota((count, queries), 0) == iota((count, queries), 1) * HEADS + at).astype(f32).astype(bf16)
+        turned = dot(rope_parts[...], order, 0, 0)
+        rope_out[at * rope:(at + 1) * rope, :] = turned[:rope] + turned[rope:]
+
     for copy in weights_far:
         copy.wait_recv()
     key_acc[1, low] = total(key_acc[1, low], key_half[0]).astype(bf16)
@@ -448,6 +430,18 @@
         copies.start(value_acc.at[3, high], value_in.at[1, high], down),
     ]
 
+    for copy in scatter:
+        copy.wait_recv()
+    parts = [z_in[0, step] for step in range(1, NZ)] + [z_in[1, step] for step in range(NZ)]
+    done[...] = total(block[x_lo, z], *parts).astype(bf16)
+    final[x_lo, z] = done[...]
+    gather = {}
+    crossed = []
+    for step in far_first:
+        gather[step] = copies.start(done, final.at[x_lo, z], z_device[step])
+        if step in direct:
+            crossed.append(copies.start(done, final.at[x_lo, z], x_device[step], cross_sems.at[step]))
+    crossed.append(copies.start(done, final.at[x_lo, z], x_pair, cross_sems.at[0]))
     def pass_on(steps):
         for step in steps:
             gather[step].wait_recv()
@@ -485,7 +479,7 @@
     value_piece = (heads, 2, latent // 16, values)
     half_key = (heads // 2,) + key_piece[1:]
     half_value = (heads // 2,) + value_piece[1:]
-    n_copies = 4 + 2 + 4 + 1 + 15 + 31 + 16
+    n_copies = 4 + 6 + 31 + 31 + 16
     vmem = pl.BlockSpec(memory_space=pltpu.VMEM)
     hbm = pl.BlockSpec(memory_space=pltpu.HBM)
     return pl.pallas_call(
@@ -510,9 +504,8 @@
             pltpu.VMEM((NY, 2, 64, width), bf16),
             pltpu.VMEM((2, 64, width), bf16),
             pltpu.VMEM((2, 2, 64, width), bf16),
-            pltpu.VMEM((64, width), bf16),
-            pltpu.VMEM((NZ, 4, width), bf16),
-            pltpu.VMEM((NZ, 4, width), bf16),
+            pltpu.VMEM((2, NZ, 4, width), bf16),
+            pltpu.VMEM((2, NZ, 4, width), bf16),
             pltpu.VMEM((4, width), bf16),
             pltpu.VMEM((heads, NY, 2) + key_piece[1:], bf16),
             pltpu.VMEM((heads, NY, 2) + value_piece[1:], bf16),
@@ -534,7 +527,6 @@
             pltpu.SemaphoreType.DMA((n_copies,)),
             pltpu.SemaphoreType.DMA((n_copies,)),
             pltpu.SemaphoreType.DMA((3,)),
-            pltpu.SemaphoreType.DMA((4,)),
             pltpu.SemaphoreType.DMA((NZ,)),
         ],
         compiler_params=pltpu.CompilerParams(

time: 65.7 us -> 64.7 us (0.985)
  the two profiles are of different devices: /device:TPU:6 before, /device:TPU:40 now
where the time goes in v6:
time: 64.7 us; the launch traced here: 64.6 us
  Pallas kernels  63.9 us (99%)
  between operations  0.65 us (1%)
    pallas_call x1, Pallas kernels, attend_and_reduce(): pl.pallas_call(main_kernel, out_shape=(pltpu.VMEM((count, n_nope), f32),...  48.1 us
    pallas_call x1, Pallas kernels, gather_and_score(): pl.pallas_call(gather_kernel, out_shape=(pltpu.VMEM((n_keys, width), bf16...  14.9 us

profile of v6, /device:TPU:40, one launch (start us, length us, event | category | flops | bytes accessed | tf_op | source)
XLA Modules:
  0.0 64.6 jit_solution(18353168230429823223)
XLA Ops:
  0.6 14.9 %shard_map.119 = (bf16[1024,576]{1,0:T(8,128)(2,1)S(1)}, bf16[512,576]{1,0:T(8,128)(2,1)S(1)}, bf16[512,512]{1,0:T(8,128)(2,1)S(1)}, f32[1024,512]{1,0:T(8,128)S...) custom-call(s32[1,16]{1,0:T(1,128)} %table_hbm.1, s32[1,128]{1,0:T(1,128)} %pos_hbm.1, bf16[128,576]{1,0:T(8,128)(2,1)} %bitcast.19, ...), custom_call_target="tpu_custom_call" | custom-call | tf_op jit(solution)/shard_map/pallas_call | solution.py:208
  15.5 48.1 %shard_map.120 = (f32[512,128]{1,0:T(8,128)S(1)}, f32[256,128]{1,0:T(8,128)S(1)}, bf16[2,16,4,576]{3,2,1,0:T(4,128)(2,1)S(1)}, f32[4,8,512]{2,1,0:T(8,128)S(1)}, f32[4,32,128]{2,1,0:T(8,128)S(1)}) custom-call(bf16[1024,576]{1,0:T(8,128)(2,1)S(1)} %get-tuple-element.21.keys_ref, bf16[512,576]{1,0:T(8,128)(2,1)S(1)} %get-tuple-element.22.query_ref, ...), custom_call_target="tpu_custom_call" | custom-call | tf_op jit(solution)/shard_map/pallas_call | solution.py:485
  63.6 0.9 %shard_map.121 = (f32[512,128]{1,0:T(8,128)}, f32[256,128]{1,0:T(8,128)}, f32[128,576]{1,0:T(8,128)}, f32[4,8,512]{2,1,0:T(8,128)}, f32[4,32,128]{2,1,0:T(8,128)}) custom-call(f32[512,128]{1,0:T(8,128)S(1)} %get-tuple-element.27.refs_0_, f32[256,128]{1,0:T(8,128)S(1)} %get-tuple-element.28.refs_1_, bf16[2,16,4,576]{3,2,1,0:T(4,128)(2,1)S(1)} %get-tuple-element.29.refs_2_, ...), custom_call_target="tpu_custom_call" | custom-call | tf_op jit(solution)/shard_map/pallas_call | solution.py:556

commit v7 on v6

--- a/solution.py
+++ b/solution.py
@@ -240,7 +240,7 @@
     pair_key, pair_value, key_acc, value_acc, key_half, value_half, key_in, value_in,
     key_sum, value_sum, key_far, value_far,
     nope_ref, grad_ref, key_up_ref,
-    send_sems, recv_sems, fetch_sems, cross_sems,
+    send_sems, recv_sems, fetch_sems,
 ):
     ctx = lax.axis_index("ctx")
     head = lax.axis_index("head")
@@ -258,7 +258,6 @@
     x_device = [{"head": (1 - x_lo) * NZ + place} for place in z_at]
     dp_pair = {"dp": 1 - dp}
     far_first = sorted(range(1, NZ), key=lambda step: -min(step, NZ - step))
-    direct = far_first[:5]
     friends = [z_device[step] for step in far_first] + [x_device[step] for step in far_first]
     friends += [x_pair, dp_pair, up, down, sibling]
     barrier = pltpu.get_barrier_semaphore()
@@ -331,6 +330,13 @@
     down_own = copies.start(acc.at[3, 0], ring_in.at[1, 0], down)
     join(0)
 
+    up_far.wait_recv()
+    acc[1, 0] = total(acc[1, 0], ring_half[0]).astype(bf16)
+    up_both = copies.start(acc.at[1, 0], ring_in.at[0, 0], up)
+    down_far.wait_recv()
+    acc[3, 1] = total(acc[3, 1], ring_half[1]).astype(bf16)
+    down_both = copies.start(acc.at[3, 1], ring_in.at[1, 1], down)
+
     @pl.loop(0, count // 128)
     def _(step):
         lane = pl.ds(pl.multiple_of(step * 128, 128), 128)
@@ -339,35 +345,6 @@
         rope_high = grad[:, latent:].astype(bf16)
         rope_parts[lane, :width - latent] = rope_high
         rope_parts[lane, width - latent:] = (grad[:, latent:] - rope_high.astype(f32)).astype(bf16)
-
-    for copy in fetches:
-        copy.wait()
-
-    @pl.loop(0, HEADS)
-    def _(at):
-        part = dot(one_head(nope_ref[...], at), query_grad[...], 0, 0)
-        key_part[at] = part.astype(bf16).reshape(key_part.shape[1:])
-
-    pair_weights = [copies.start(key_part.at[:, :, 1 - core], pair_key, sibling)]
-
-    up_far.wait_recv()
-    acc[1, 0] = total(acc[1, 0], ring_half[0]).astype(bf16)
-    up_both = copies.start(acc.at[1, 0], ring_in.at[0, 0], up)
-    down_far.wait_recv()
-    acc[3, 1] = total(acc[3, 1], ring_half[1]).astype(bf16)
-    down_both = copies.start(acc.at[3, 1], ring_in.at[1, 1], down)
-
-    @pl.loop(0, latent // 128)
-    def _(step):
-        lane = pl.ds(pl.multiple_of(step * 128, 128), 128)
-        out_t[lane, :] = dot(keys_ref[:, lane], prob_t[...], 0, 0).astype(bf16)
-
-    @pl.loop(0, HEADS)
-    def _(at):
-        part = dot(out_t[...], one_head(grad_ref[...], at), 1, 0)
-        value_part[at] = part.astype(bf16).reshape(value_part.shape[1:])
-
-    pair_weights.append(copies.start(value_part.at[:, :, 1 - core], pair_value, sibling))
 
     for copy in (up_own, down_own, up_both, down_both):
         copy.wait_recv()
@@ -382,24 +359,46 @@
             scatter.append(copies.start(block.at[x_lo, z_at[step]], z_in.at[0, step], z_device[step]))
         scatter.append(copies.start(block.at[1 - x_lo, z_at[step]], z_in.at[1, step], x_device[step]))
 
-    for copy in pair_weights:
-        copy.wait_recv()
-    for step in range(NY):
-        key_acc[step] = total(key_part[:, chips[step], core], pair_key[:, chips[step]]).astype(bf16)
-        value_acc[step] = total(value_part[:, chips[step], core], pair_value[:, chips[step]]).astype(bf16)
+    for copy in fetches:
+        copy.wait()
+
+    @pl.loop(0, HEADS)
+    def _(at):
+        part = dot(one_head(nope_ref[...], at), query_grad[...], 0, 0)
+        key_part[at] = part.astype(bf16).reshape(key_part.shape[1:])
+
+    pair_weights = [copies.start(key_part.at[:, :, 1 - core], pair_key, sibling)]
+
+    @pl.loop(0, latent // 128)
+    def _(step):
+        lane = pl.ds(pl.multiple_of(step * 128, 128), 128)
+        out_t[lane, :] = dot(keys_ref[:, lane], prob_t[...], 0, 0).astype(bf16)
+
+    @pl.loop(0, HEADS)
+    def _(at):
+        part = dot(out_t[...], one_head(grad_ref[...], at), 1, 0)
+        value_part[at] = part.astype(bf16).reshape(value_part.shape[1:])
+
+    pair_weights.append(copies.start(value_part.at[:, :, 1 - core], pair_value, sibling))
+
+    weights_far, weights_in = [], []
     low, high = pl.ds(0, 2), pl.ds(2, 2)
-    weights_far = [
-        copies.start(key_acc.at[2, low], key_half.at[0], up),
-        copies.start(value_acc.at[2, low], value_half.at[0], up),
-        copies.start(key_acc.at[2, high], key_half.at[1], down),
-        copies.start(value_acc.at[2, high], value_half.at[1], down),
-    ]
-    weights_in = [
-        copies.start(key_acc.at[1, high], key_in.at[0, high], up),
-        copies.start(value_acc.at[1, high], value_in.at[0, high], up),
-        copies.start(key_acc.at[3, low], key_in.at[1, low], down),
-        copies.start(value_acc.at[3, low], value_in.at[1, low], down),
-    ]
+    weights = (
+        (pair_weights[0], key_part, pair_key, key_acc, key_half, key_in),
+        (pair_weights[1], value_part, pair_value, value_acc, value_half, value_in),
+    )
+    for copy, part, paired, joined, half_in, ring_to in weights:
+        copy.wait_recv()
+        for step in (2, 1, 3, 0):
+            joined[step] = total(part[:, chips[step], core], paired[:, chips[step]]).astype(bf16)
+            if step == 2:
+                weights_far.append(copies.start(joined.at[2, low], half_in.at[0], up))
+                weights_far.append(copies.start(joined.at[2, high], half_in.at[1], down))
+            if step == 1:
+                weights_in.append(copies.start(joined.at[1, high], ring_to.at[0, high], up))
+            if step == 3:
+                weights_in.append(copies.start(joined.at[3, low], ring_to.at[1, low], down))
+
     @pl.loop(0, count // 128)
     def _(step):
         rows = pl.ds(step * 128, 128)
@@ -416,6 +415,17 @@
         order = (iota((count, queries), 0) == iota((count, queries), 1) * HEADS + at).astype(f32).astype(bf16)
         turned = dot(rope_parts[...], order, 0, 0)
         rope_out[at * rope:(at + 1) * rope, :] = turned[:rope] + turned[rope:]
+
+    for copy in scatter:
+        copy.wait_recv()
+    parts = [z_in[0, step] for step in range(1, NZ)] + [z_in[1, step] for step in range(NZ)]
+    done[...] = total(block[x_lo, z], *parts).astype(bf16)
+    final[x_lo, z] = done[...]
+    gather = []
+    for step in far_first + [0]:
+        if step:
+            gather.append(copies.start(done, final.at[x_lo, z], z_device[step]))
+        gather.append(copies.start(done, final.at[x_lo, z], x_device[step]))
 
     for copy in weights_far:
         copy.wait_recv()
@@ -430,28 +440,6 @@
         copies.start(value_acc.at[3, high], value_in.at[1, high], down),
     ]
 
-    for copy in scatter:
-        copy.wait_recv()
-    parts = [z_in[0, step] for step in range(1, NZ)] + [z_in[1, step] for step in range(NZ)]
-    done[...] = total(block[x_lo, z], *parts).astype(bf16)
-    final[x_lo, z] = done[...]
-    gather = {}
-    crossed = []
-    for step in far_first:
-        gather[step] = copies.start(done, final.at[x_lo, z], z_device[step])
-        if step in direct:
-            crossed.append(copies.start(done, final.at[x_lo, z], x_device[step], cross_sems.at[step]))
-    crossed.append(copies.start(done, final.at[x_lo, z], x_pair, cross_sems.at[0]))
-    def pass_on(steps):
-        for step in steps:
-            gather[step].wait_recv()
-            if step not in direct:
-                come = final.at[x_lo, z_at[NZ - step]]
-                crossed.append(copies.start(come, come, x_pair, cross_sems.at[step]))
-
-    near_first = far_first[::-1]
-    pass_on(near_first[:6])
-
     for copy in weights_in:
         copy.wait_recv()
     key_sum[...] = total(key_acc[0], key_in[0], key_in[1]).astype(bf16)
@@ -460,12 +448,11 @@
         copies.start(key_sum.at[:, 1 - dp], key_far, dp_pair),
         copies.start(value_sum.at[:, 1 - dp], value_far, dp_pair),
     ]
-    pass_on(near_first[6:])
     for copy in weights_pair:
         copy.wait_recv()
     key_out[...] = total(key_sum[:, dp], key_far[...])
     value_out[...] = total(value_sum[:, dp], value_far[...])
-    for copy in crossed:
+    for copy in gather:
         copy.wait_recv()
     copies.finish()
 
@@ -527,7 +514,6 @@
             pltpu.SemaphoreType.DMA((n_copies,)),
             pltpu.SemaphoreType.DMA((n_copies,)),
             pltpu.SemaphoreType.DMA((3,)),
-            pltpu.SemaphoreType.DMA((NZ,)),
         ],
         compiler_params=pltpu.CompilerParams(
             collective_id=1, has_side_effects=True, vmem_limit_bytes=VMEM_LIMIT

time: 64.7 us -> 62.7 us (0.969)
  the two profiles are of different devices: /device:TPU:40 before, /device:TPU:6 now
where the time goes in v7:
time: 62.7 us; the launch traced here: 61.5 us
  Pallas kernels  60.9 us (97%)
  between operations  0.65 us (1%)
    pallas_call x1, Pallas kernels, attend_and_reduce(): pl.pallas_call(main_kernel, out_shape=(pltpu.VMEM((count, n_nope), f32),...  43.8 us
    pallas_call x1, Pallas kernels, gather_and_score(): pl.pallas_call(gather_kernel, out_shape=(pltpu.VMEM((n_keys, width), bf16...  16.1 us

profile of v7, /device:TPU:6, one launch (start us, length us, event | category | flops | bytes accessed | tf_op | source)
XLA Modules:
  0.0 61.5 jit_solution(2542464415123946043)
XLA Ops:
  0.6 16.1 %shard_map.119 = (bf16[1024,576]{1,0:T(8,128)(2,1)S(1)}, bf16[512,576]{1,0:T(8,128)(2,1)S(1)}, bf16[512,512]{1,0:T(8,128)(2,1)S(1)}, f32[1024,512]{1,0:T(8,128)S...) custom-call(s32[1,16]{1,0:T(1,128)} %table_hbm.1, s32[1,128]{1,0:T(1,128)} %pos_hbm.1, bf16[128,576]{1,0:T(8,128)(2,1)} %bitcast.19, ...), custom_call_target="tpu_custom_call" | custom-call | tf_op jit(solution)/shard_map/pallas_call | solution.py:208
  16.8 43.8 %shard_map.120 = (f32[512,128]{1,0:T(8,128)S(1)}, f32[256,128]{1,0:T(8,128)S(1)}, bf16[2,16,4,576]{3,2,1,0:T(4,128)(2,1)S(1)}, f32[4,8,512]{2,1,0:T(8,128)S(1)}, f32[4,32,128]{2,1,0:T(8,128)S(1)}) custom-call(bf16[1024,576]{1,0:T(8,128)(2,1)S(1)} %get-tuple-element.21.keys_ref, bf16[512,576]{1,0:T(8,128)(2,1)S(1)} %get-tuple-element.22.query_ref, ...), custom_call_target="tpu_custom_call" | custom-call | tf_op jit(solution)/shard_map/pallas_call | solution.py:472
  60.6 0.9 %shard_map.121 = (f32[512,128]{1,0:T(8,128)}, f32[256,128]{1,0:T(8,128)}, f32[128,576]{1,0:T(8,128)}, f32[4,8,512]{2,1,0:T(8,128)}, f32[4,32,128]{2,1,0:T(8,128)}) custom-call(f32[512,128]{1,0:T(8,128)S(1)} %get-tuple-element.27.refs_0_, f32[256,128]{1,0:T(8,128)S(1)} %get-tuple-element.28.refs_1_, bf16[2,16,4,576]{3,2,1,0:T(4,128)(2,1)S(1)} %get-tuple-element.29.refs_2_, ...), custom_call_target="tpu_custom_call" | custom-call | tf_op jit(solution)/shard_map/pallas_call | solution.py:542

commit v8 on v4

--- a/solution.py
+++ b/solution.py
@@ -74,14 +74,14 @@
 
 
 def gather_kernel(
-    table_ref, pos_ref, own_ref, nope_hbm, grad_hbm, rope_hbm, key_up_hbm, value_up_hbm,
+    table_hbm, pos_hbm, own_ref, nope_hbm, grad_hbm, rope_hbm, key_up_hbm, value_up_hbm,
     all_ref, query_ref, latent_ref, scores, grad_probs, row_max,
-    nope_ref, grad_ref, rope_ref, key_up_ref, value_up_ref,
+    table_ref, pos_ref, nope_ref, grad_ref, rope_ref, key_up_ref, value_up_ref,
     send_sems, recv_sems, own_sem, fetch_sems,
 ):
     fetches = fetch(
-        [nope_hbm, key_up_hbm, rope_hbm, grad_hbm, value_up_hbm],
-        [nope_ref, key_up_ref, rope_ref, grad_ref, value_up_ref],
+        [nope_hbm, key_up_hbm, rope_hbm, grad_hbm, value_up_hbm, table_hbm, pos_hbm],
+        [nope_ref, key_up_ref, rope_ref, grad_ref, value_up_ref, table_ref, pos_ref],
         fetch_sems,
     )
     ctx = lax.axis_index("ctx")
@@ -104,11 +104,8 @@
     entry_barrier([sibling, at(1, core), at(3, core)])
     copies = Copies(send_sems, recv_sems)
     halves = range(2)
-    to_ahead, to_behind = [], []
-    for part in halves:
-        mine = own_ref.at[pl.ds(part * half, half)]
-        to_ahead.append(copies.start(mine, slot(0, part), at(ahead, core)))
-        to_behind.append(copies.start(mine, slot(0, part), at(behind, core)))
+    own_half = [own_ref.at[pl.ds(part * half, half)] for part in halves]
+    to_ahead = [copies.start(own_half[part], slot(0, part), at(ahead, core)) for part in halves]
     own_slot = all_ref.at[pl.ds(place(0, core), rows_each)]
     pair_own = copies.start(own_ref, own_slot, sibling)
     keep = pltpu.make_async_copy(own_ref, own_slot, own_sem)
@@ -139,14 +136,13 @@
         copy.wait()
     project(0)
     project(1)
+    to_behind = [copies.start(own_half[part], slot(0, part), at(behind, core)) for part in halves]
     project(2)
-    onward, from_behind, from_ahead = [], [], []
+    onward, from_behind = [], []
     for part in halves:
         to_ahead[part].wait_recv()
         onward.append(copies.start(slot(behind, part), slot(behind, part), at(ahead, core)))
         from_behind.append(copies.start(slot(behind, part), slot(behind, part), sibling))
-        to_behind[part].wait_recv()
-        from_ahead.append(copies.start(slot(ahead, part), slot(ahead, part), sibling))
         if part == 0:
             project(3)
 
@@ -179,12 +175,16 @@
     score(all_ref, place(0, core), place(0, core))
     pair_own.wait_recv()
     score(all_ref, place(0, 1 - core), place(0, 1 - core))
+    from_ahead = []
+    for part in halves:
+        to_behind[part].wait_recv()
+        from_ahead.append(copies.start(slot(ahead, part), slot(ahead, part), sibling))
     score(all_ref, place(behind, core), place(behind, core))
-    onward[0].wait_recv()
-    far = [copies.start(slot(2, 0), slot(2, 0), sibling)]
+    far = []
+    for part in halves:
+        onward[part].wait_recv()
+        far.append(copies.start(slot(2, part), slot(2, part), sibling))
     score(all_ref, place(ahead, core), place(ahead, core))
-    onward[1].wait_recv()
-    far.append(copies.start(slot(2, 1), slot(2, 1), sibling))
     for copy in from_behind:
         copy.wait_recv()
     score(all_ref, place(ahead, 1 - core), place(ahead, 1 - core))
@@ -215,14 +215,15 @@
             pltpu.VMEM((n_keys, count), f32),
             pltpu.VMEM((1, count), f32),
         ),
-        in_specs=[pl.BlockSpec(memory_space=pltpu.SMEM), vmem] + [hbm] * 6,
+        in_specs=[hbm] * 8,
         out_specs=(vmem,) * 6,
-        scratch_shapes=[pltpu.VMEM(array.shape, bf16) for array in (nope, grad, rope, key_up, value_up)]
+        scratch_shapes=[pltpu.SMEM(table.shape, jnp.int32), pltpu.VMEM(pos.shape, jnp.int32)]
+        + [pltpu.VMEM(array.shape, bf16) for array in (nope, grad, rope, key_up, value_up)]
         + [
             pltpu.SemaphoreType.DMA((13,)),
             pltpu.SemaphoreType.DMA((13,)),
             pltpu.SemaphoreType.DMA,
-            pltpu.SemaphoreType.DMA((5,)),
+            pltpu.SemaphoreType.DMA((7,)),
         ],
         compiler_params=pltpu.CompilerParams(
             collective_id=0, has_side_effects=True, vmem_limit_bytes=VMEM_LIMIT
@@ -369,23 +370,6 @@
 
     pair_weights.append(copies.start(value_part.at[:, :, 1 - core], pair_value, sibling))
 
-    @pl.loop(0, count // 128)
-    def _(step):
-        rows = pl.ds(step * 128, 128)
-        every = dot(query_grad[rows, :], key_up_ref[...].reshape(-1, latent), 1, 1)
-        n = nope_out.shape[1]
-        which = lax.rem(iota((128, n), 0), HEADS)
-        nope_out[rows, :] = total(
-            *[jnp.where(which == at, every[:, at * n:(at + 1) * n], 0.0) for at in range(HEADS)]
-        )
-
-    rope = width - latent
-    queries = count // HEADS
-    for at in range(HEADS):
-        order = (iota((count, queries), 0) == iota((count, queries), 1) * HEADS + at).astype(f32).astype(bf16)
-        turned = dot(rope_parts[...], order, 0, 0)
-        rope_out[at * rope:(at + 1) * rope, :] = turned[:rope] + turned[rope:]
-
     for copy in pair_weights:
         copy.wait_recv()
     for step in range(NY):
@@ -404,6 +388,23 @@
         copies.start(key_acc.at[3, low], key_in.at[1, low], down),
         copies.start(value_acc.at[3, low], value_in.at[1, low], down),
     ]
+    @pl.loop(0, count // 128)
+    def _(step):
+        rows = pl.ds(step * 128, 128)
+        every = dot(query_grad[rows, :], key_up_ref[...].reshape(-1, latent), 1, 1)
+        n = nope_out.shape[1]
+        which = lax.rem(iota((128, n), 0), HEADS)
+        nope_out[rows, :] = total(
+            *[jnp.where(which == at, every[:, at * n:(at + 1) * n], 0.0) for at in range(HEADS)]
+        )
+
+    rope = width - latent
+    queries = count // HEADS
+    for at in range(HEADS):
+        order = (iota((count, queries), 0) == iota((count, queries), 1) * HEADS + at).astype(f32).astype(bf16)
+        turned = dot(rope_parts[...], order, 0, 0)
+        rope_out[at * rope:(at + 1) * rope, :] = turned[:rope] + turned[rope:]
+
     for copy in scatter:
         copy.wait_recv()
     piece[...] = total(block[z], *[z_in[step] for step in range(1, NZ)]).astype(bf16)

time: 62 us -> 62.3 us (level)
  no operation moved by 1% of the time
where the time goes in v8:
time: 62.3 us; the launch traced here: 61.7 us
  Pallas kernels  61.1 us (98%)
  between operations  0.65 us (1%)
    pallas_call x1, Pallas kernels, attend_and_reduce(): pl.pallas_call(main_kernel, out_shape=(pltpu.VMEM((count, n_nope), f32),...  44 us
    pallas_call x1, Pallas kernels, gather_and_score(): pl.pallas_call(gather_kernel, out_shape=(pltpu.VMEM((n_keys, width), bf16...  16.1 us

profile of v8, /device:TPU:6, one launch (start us, length us, event | category | flops | bytes accessed | tf_op | source)
XLA Modules:
  0.0 61.7 jit_solution(6953366778514798913)
XLA Ops:
  0.6 16.1 %shard_map.119 = (bf16[1024,576]{1,0:T(8,128)(2,1)S(1)}, bf16[512,576]{1,0:T(8,128)(2,1)S(1)}, bf16[512,512]{1,0:T(8,128)(2,1)S(1)}, f32[1024,512]{1,0:T(8,128)S...) custom-call(s32[1,16]{1,0:T(1,128)} %table_hbm.1, s32[1,128]{1,0:T(1,128)} %pos_hbm.1, bf16[128,576]{1,0:T(8,128)(2,1)} %bitcast.19, ...), custom_call_target="tpu_custom_call" | custom-call | tf_op jit(solution)/shard_map/pallas_call | solution.py:208
  16.8 44.0 %shard_map.120 = (f32[512,128]{1,0:T(8,128)S(1)}, f32[256,128]{1,0:T(8,128)S(1)}, bf16[16,8,576]{2,1,0:T(8,128)(2,1)S(1)}, f32[4,8,512]{2,1,0:T(8,128)S(1)}, f32[4,32,128]{2,1,0:T(8,128)S(1)}) custom-call(bf16[1024,576]{1,0:T(8,128)(2,1)S(1)} %get-tuple-element.21.keys_ref, bf16[512,576]{1,0:T(8,128)(2,1)S(1)} %get-tuple-element.22.query_ref, ...), custom_call_target="tpu_custom_call" | custom-call | tf_op jit(solution)/shard_map/pallas_call | solution.py:459
  60.8 0.9 %shard_map.121 = (f32[512,128]{1,0:T(8,128)}, f32[256,128]{1,0:T(8,128)}, f32[16,8,576]{2,1,0:T(8,128)}, f32[4,8,512]{2,1,0:T(8,128)}, f32[4,32,128]{2,1,0:T(8,128)}) custom-call(f32[512,128]{1,0:T(8,128)S(1)} %get-tuple-element.27.refs_0_, f32[256,128]{1,0:T(8,128)S(1)} %get-tuple-element.28.refs_1_, bf16[16,8,576]{2,1,0:T(8,128)(2,1)S(1)} %get-tuple-element.29.refs_2_, ...), custom_call_target="tpu_custom_call" | custom-call | tf_op jit(solution)/shard_map/pallas_call | solution.py:524

commit v9 on v8

--- a/solution.py
+++ b/solution.py
@@ -231,6 +231,12 @@
     )(table, pos, own_rows, nope, grad, rope, key_up, value_up)
 
 
+def tiles_of(rows):
+    wide = rows.shape[1] // 128
+    tiles = [rows[top:top + 4, lane * 128:lane * 128 + 128] for lane in range(wide) for top in (0, 4)]
+    return tiles + [jnp.concatenate([rows[0:4, wide * 128:], rows[4:8, wide * 128:]], axis=1)]
+
+
 def main_kernel(
     keys_ref, query_ref, latent_ref, scores, grad_probs, row_max_ref, nope_hbm, grad_hbm, key_up_hbm,
     nope_out, rope_out, final, key_out, value_out,
@@ -345,7 +351,11 @@
 
     for copy in (up_own, down_own, up_both, down_both):
         copy.wait_recv()
-    block[...] = total(acc[0], ring_in[0], ring_in[1]).astype(bf16).reshape(block.shape)
+    for half in range(2):
+        mine = total(acc[0, half], ring_in[0, half], ring_in[1, half])
+        for at in range(NZ // 2):
+            for tile, part in enumerate(tiles_of(mine[at * 8:at * 8 + 8])):
+                block[half * (NZ // 2) + at, tile] = part.astype(bf16)
     scatter = [copies.start(block.at[z_at[step]], z_in.at[step], z_device[step]) for step in far_first]
 
     for copy in fetches:
@@ -453,6 +463,7 @@
     value_piece = (heads, 2, latent // 16, values)
     half_key = (heads // 2,) + key_piece[1:]
     half_value = (heads // 2,) + value_piece[1:]
+    packed = (8 * width // 512, 4, 128)
     n_copies = 4 + 2 + 6 + 8 + 4 + 15 + 1 + 2 + 15
     vmem = pl.BlockSpec(memory_space=pltpu.VMEM)
     hbm = pl.BlockSpec(memory_space=pltpu.HBM)
@@ -461,7 +472,7 @@
         out_shape=(
             pltpu.VMEM((count, n_nope), f32),
             pltpu.VMEM((heads * (width - latent), count // heads), f32),
-            pltpu.VMEM((NZ, 8, width), bf16),
+            pltpu.VMEM((NZ,) + packed, bf16),
             pltpu.VMEM((heads, n_nope // 16, latent), f32),
             pltpu.VMEM((heads, latent // 16, values), f32),
         ),
@@ -478,11 +489,11 @@
             pltpu.VMEM((NY, 2, 64, width), bf16),
             pltpu.VMEM((2, 64, width), bf16),
             pltpu.VMEM((2, 2, 64, width), bf16),
-            pltpu.VMEM((NZ, 8, width), bf16),
-            pltpu.VMEM((NZ, 8, width), bf16),
-            pltpu.VMEM((8, width), bf16),
-            pltpu.VMEM((8, width), bf16),
-            pltpu.VMEM((8, width), bf16),
+            pltpu.VMEM((NZ,) + packed, bf16),
+            pltpu.VMEM((NZ,) + packed, bf16),
+            pltpu.VMEM(packed, bf16),
+            pltpu.VMEM(packed, bf16),
+            pltpu.VMEM(packed, bf16),
             pltpu.VMEM((heads, NY, 2) + key_piece[1:], bf16),
             pltpu.VMEM((heads, NY, 2) + value_piece[1:], bf16),
             pltpu.VMEM((heads, NY) + key_piece[1:], bf16),
@@ -516,14 +527,29 @@
 
 def store_kernel(*refs):
     for source, target in zip(refs[:5], refs[5:10]):
-        target[...] = source[...].astype(f32)
+        if source.dtype != bf16:
+            target[...] = source[...]
+            continue
+        for piece in range(source.shape[0]):
+            for top in (0, 4):
+                rows = slice(piece * 8 + top, piece * 8 + top + 4)
+                wide = source.shape[1] // 2
+                for lane in range(wide):
+                    target[rows, lane * 128:lane * 128 + 128] = source[piece, 2 * lane + top // 4].astype(f32)
+                last = source[piece, 2 * wide].astype(f32)
+                target[rows, wide * 128:] = last[:, top * 16:top * 16 + 64]
 
 
 def store_results(*results):
     vmem = pl.BlockSpec(memory_space=pltpu.VMEM)
     return pl.pallas_call(
         store_kernel,
-        out_shape=tuple(jax.ShapeDtypeStruct(result.shape, f32) for result in results),
+        out_shape=tuple(
+            jax.ShapeDtypeStruct(
+                result.shape if result.dtype != bf16 else (result.shape[0] * 8, result.shape[1] * 64), f32
+            )
+            for result in results
+        ),
         in_specs=[vmem] * len(results),
         out_specs=(vmem,) * len(results),
         compiler_params=pltpu.CompilerParams(vmem_limit_bytes=VMEM_LIMIT),

time: 62.3 us -> 61.9 us (level)
  Pallas kernels: 61.1 us -> 60.1 us
    pallas_call x1, Pallas kernels: 44 us -> 43.1 us  [attend_and_reduce(): pl.pallas_call(main_kernel, out_shape=(pltpu.VMEM((count, n_nope), f32),...]
where the time goes in v9:
time: 61.9 us; the launch traced here: 60.8 us
  Pallas kernels  60.1 us (97%)
  between operations  0.65 us (1%)
    pallas_call x1, Pallas kernels, attend_and_reduce(): pl.pallas_call(main_kernel, out_shape=(pltpu.VMEM((count, n_nope), f32),...  43.1 us
    pallas_call x1, Pallas kernels, gather_and_score(): pl.pallas_call(gather_kernel, out_shape=(pltpu.VMEM((n_keys, width), bf16...  16.1 us

profile of v9, /device:TPU:6, one launch (start us, length us, event | category | flops | bytes accessed | tf_op | source)
XLA Modules:
  0.0 60.8 jit_solution(11122320162934791949)
XLA Ops:
  0.6 16.1 %shard_map.119 = (bf16[1024,576]{1,0:T(8,128)(2,1)S(1)}, bf16[512,576]{1,0:T(8,128)(2,1)S(1)}, bf16[512,512]{1,0:T(8,128)(2,1)S(1)}, f32[1024,512]{1,0:T(8,128)S...) custom-call(s32[1,16]{1,0:T(1,128)} %table_hbm.1, s32[1,128]{1,0:T(1,128)} %pos_hbm.1, bf16[128,576]{1,0:T(8,128)(2,1)} %bitcast.19, ...), custom_call_target="tpu_custom_call" | custom-call | tf_op jit(solution)/shard_map/pallas_call | solution.py:208
  16.8 43.1 %shard_map.120 = (f32[512,128]{1,0:T(8,128)S(1)}, f32[256,128]{1,0:T(8,128)S(1)}, bf16[16,9,4,128]{3,2,1,0:T(4,128)(2,1)S(1)}, f32[4,8,512]{2,1,0:T(8,128)S(1)}, f32[4,32,128]{2,1,0:T(8,128)S(1)}) custom-call(bf16[1024,576]{1,0:T(8,128)(2,1)S(1)} %get-tuple-element.21.keys_ref, bf16[512,576]{1,0:T(8,128)(2,1)S(1)} %get-tuple-element.22.query_ref, ...), custom_call_target="tpu_custom_call" | custom-call | tf_op jit(solution)/shard_map/pallas_call | solution.py:470
  59.9 0.9 %shard_map.121 = (f32[512,128]{1,0:T(8,128)}, f32[256,128]{1,0:T(8,128)}, f32[128,576]{1,0:T(8,128)}, f32[4,8,512]{2,1,0:T(8,128)}, f32[4,32,128]{2,1,0:T(8,128)}) custom-call(f32[512,128]{1,0:T(8,128)S(1)} %get-tuple-element.27.refs_0_, f32[256,128]{1,0:T(8,128)S(1)} %get-tuple-element.28.refs_1_, bf16[16,9,4,128]{3,2,1,0:T(4,128)(2,1)S(1)} %get-tuple-element.29.refs_2_, ...), custom_call_target="tpu_custom_call" | custom-call | tf_op jit(solution)/shard_map/pallas_call | solution.py:545
